TPU v7x, 128 devices: a whole 4x4x4 slice. The times are simulated.
128 devices in a mesh: pat: 2 (over x_lo), gx: 64 (over z, x_hi, y, core).
Axes of the slice: x: 4 (x_hi: 2, x_lo: 2; x = x_hi * 2 + x_lo), y: 4, z: 4, core: 2. Of those that a mesh axis runs over, the one named last changes fastest.
Arguments:
- pattern_index: int32 [2], P('pat'), may hold values from 0 to 7
- patterns: float32 [8, 512, 1024], P(None, 'gx'), may hold values from -6 to 6
- freq_bins: int32 [16], replicated, may hold values from 0 to 511
- absorption: float32 [512, 1024, 128], P('gx'), may hold values from 0.05 to 0.5
- forward_start: float32 [2, 512, 1024, 128], P('pat', 'gx'), may hold values from -6 to 6
- adjoint_start: float32 [2, 512, 1024, 128], P('pat', 'gx'), may hold values from -6 to 6
- measured: float32 [2, 2, 16, 1024], P('pat', None, None, 'gx'), may hold values from -6 to 6
Outputs:
- gradient: float32 [512, 1024, 128], P('gx', 'pat')
- model: float32 [2, 2, 16, 1024], P('pat', None, None, 'gx')
All inputs are finite; a program needn't handle non-finite values.
Results may differ from a plain program's by a relative error of at most 0.00029.
Values sent between devices are 32-bit elements; how exact they have to be, the bound alone decides.
No kernel may reach another device: no remote copies, remote signals or barrier semaphores. Data moves between devices by JAX's collectives and lax.ppermute only.
A program may use at most 128 MiB of HBM per device.

v0:
```python
import math

import jax
import jax.numpy as jnp
from jax import lax
from jax.sharding import Mesh
from jax.sharding import PartitionSpec as P

SWEEPS = 4
GX = ("gx_0", "gx_1", "gx_2", "gx_3")


def extended(block, sides, width):
    for axis, dim in sides:
        count = lax.axis_size(axis)
        forward = [(i, i + 1) for i in range(count - 1)]
        backward = [(target, source) for source, target in forward]
        low = lax.ppermute(
            lax.slice_in_dim(block, block.shape[dim] - width, None, axis=dim), axis, forward
        )
        high = lax.ppermute(lax.slice_in_dim(block, 0, width, axis=dim), axis, backward)
        block = jnp.concatenate([low, block, high], axis=dim)
    return block


def split_up(array, dim, size):
    before, after = (array.shape[:dim], array.shape[dim + 1 :])
    return jnp.moveaxis(array.reshape(*before, size, -1, *after), dim, 0)


def in_order(pieces, dim):
    dims = list(pieces.shape[1:])
    dims[dim] *= pieces.shape[0]
    return jnp.moveaxis(pieces, 0, dim).reshape(dims)


def moved_by_axis(pieces, axes, turns):
    inside = pieces.shape[1:]
    filled = pieces.reshape(*(lax.axis_size(a) for a in axes), *inside)
    for k in turns:
        filled = lax.all_to_all(filled, axes[k], k, k, tiled=True)
    return filled.reshape(-1, *inside)


def core_and_chips(array, groups, turns, split_dim, concat_dim):
    size = lax.axis_size(groups[0]) * lax.axis_size(groups[1])
    pieces = split_up(array, split_dim, size)
    return in_order(moved_by_axis(pieces, groups, turns), concat_dim)


def sum_at_owner(array, axis, dim):
    pieces = split_up(array, dim, lax.axis_size(axis))
    arrived = lax.all_to_all(pieces, axis, split_axis=0, concat_axis=0, tiled=True)
    return arrived.sum(axis=0)


def sweep_weight(sweep):
    return 1.0 / (1.25 + 0.75 * math.cos(math.pi * (2 * sweep + 1) / (2 * SWEEPS)))


def relax_step(padded, source, diag, weight, depth_mask):
    inner = padded[:, 1:-1]
    side = jnp.pad(inner, ((0, 0), (0, 0), (1, 1), (1, 1)))
    beside_all = padded[:, 2:] + padded[:, :-2]
    beside_all = beside_all + side[:, :, 2:, 1:-1] + side[:, :, :-2, 1:-1]
    beside_all = beside_all + side[:, :, 1:-1, 2:] + side[:, :, 1:-1, :-2]
    drive = source[..., None] * depth_mask - (diag * inner - beside_all)
    return inner + weight * drive / diag


def solve_near(start, source, diag, depth_mask):
    field = start
    for sweep in range(SWEEPS):
        padded = extended(field, ((GX, 1),), 1)
        field = relax_step(padded, source, diag, sweep_weight(sweep), depth_mask)
    return field


def make_tables(freq_bins, positions, total_x):
    phase = freq_bins[:, None] * positions[None, :] % total_x
    angle = 2.0 * math.pi / total_x * phase.astype(jnp.float32)
    return (jnp.cos(angle) / math.sqrt(total_x), jnp.sin(angle) / math.sqrt(total_x))


def shards(pattern_index, patterns, freq_bins, absorption, forward_start, adjoint_start, measured):
    high = lax.Precision.HIGHEST
    planes = forward_start.shape[1]
    depth = forward_start.shape[3]
    total_x = lax.axis_size(GX) * planes
    selector = (
        pattern_index[:, None] == jnp.arange(patterns.shape[0], dtype=jnp.int32)[None, :]
    ).astype(jnp.float32)
    depth_mask = (jnp.arange(depth) == 0).astype(jnp.float32)
    diag = 6.0 + absorption
    source = jnp.einsum("gt,txy->gxy", selector, patterns, precision=high)
    fluence = solve_near(forward_start, source, diag, depth_mask)
    surface = fluence[:, :, :, 0]
    columns = core_and_chips(surface, (("gx_0", "gx_1", "gx_2"), "gx_3"), (1, 0), 2, 1)
    positions = jnp.arange(total_x, dtype=jnp.int32)
    cos_table, sin_table = make_tables(freq_bins, positions, total_x)
    real_part = jnp.einsum("kx,gxy->gky", cos_table, columns, precision=high)
    imag_part = -jnp.einsum("kx,gxy->gky", sin_table, columns, precision=high)
    model = jnp.stack([real_part, imag_part], axis=1)
    misfit = model - measured
    back_columns = jnp.einsum("kx,gky->gxy", cos_table, misfit[:, 0], precision=high) - jnp.einsum(
        "kx,gky->gxy", sin_table, misfit[:, 1], precision=high
    )
    adjoint_source = core_and_chips(back_columns, (("gx_0", "gx_1", "gx_2"), "gx_3"), (1, 0), 1, 2)
    adjoint = solve_near(adjoint_start, adjoint_source, diag, depth_mask)
    local_terms = -jnp.sum(fluence * adjoint, axis=0)
    gradient = sum_at_owner(local_terms, "pat", 1)
    return (gradient, model)


def solution(mesh):
    torus = Mesh(
        mesh.devices.reshape(mesh.shape["pat"], 4, 2, 4, 2), ("pat", "gx_0", "gx_1", "gx_2", "gx_3")
    )
    in_specs = (
        P("pat"),
        P(None, GX, None),
        P(),
        P(GX, None, None),
        P("pat", GX, None, None),
        P("pat", GX, None, None),
        P("pat", None, None, GX),
    )
    out_specs = (P(GX, "pat", None), P("pat", None, None, GX))
    return jax.shard_map(
        shards, mesh=torus, in_specs=in_specs, out_specs=out_specs, check_vma=False
    )
```

profile of v0, /device:TPU:32, one launch (start us, length us, event | category | flops | bytes accessed | tf_op | source)
XLA Modules:
  0.0 287.9 jit_solution(3879322076948161596)
XLA Ops:
  0.6 1.3 fusion.125
  2.0 6.4 %collective-permute-start = (f32[1,1,1024,128]{3,2,1,0:T(8,128)S(1)}, f32[1,1,1024,128]{3,2,1,0:T(8,128)S(1)}, u32[]{:S(2)}, u32[]{:S(2)}) collective-permute-start(f32[1,1,1024,128]{3,2,1,0:T(8,128)S(1)} %get-tuple-element.24), channel_id=1, source_target_pairs={{1,0},{2,1},{3,2},{4,3},{5,4},{6,5},{7,6},{8,7},{9,8},{10,9},{11,1... | collective-permute-start | bytes 1572872 | tf_op jit(solution)/shard_map/ppermute | solution.py:21
  8.3 1.9 collective-permute-start.1
  11.3 3.7 %collective-permute-done = f32[1,1,1024,128]{3,2,1,0:T(8,128)S(1)} collective-permute-done((f32[1,1,1024,128]{3,2,1,0:T(8,128)S(1)}, f32[1,1,1024,128]{3,2,1,0:T(8,128)S(1)}, u32[]{:S(2)}, u32[]{:S(2)}) %collective-permute-start) | collective-permute-done | bytes 524320 | tf_op jit(solution)/shard_map/ppermute | solution.py:21
  15.0 8.3 %collective-permute-done.1 = f32[1,1,1024,128]{3,2,1,0:T(8,128)S(1)} collective-permute-done((f32[1,1,1024,128]{3,2,1,0:T(8,128)S(1)}, f32[1,1,1024,128]{3,2,1,0:T(8,128)S(1)}, u32[]{:S(2)}, u32[]{:S(2)}) %collective-permute-start.1) | collective-permute-done | bytes 524320 | tf_op jit(solution)/shard_map/ppermute | solution.py:18
  23.4 14.1 %fusion.2 = f32[1,8,1024,128]{3,2,1,0:T(8,128)S(1)} fusion(f32[1,8,1024,128]{3,2,1,0:T(8,128)} %param.11, f32[1,1,1024,128]{3,2,1,0:T(8,128)S(1)} %collective-permute-done.1, f32[1,1,1024,128]{3,2,1,0:T(8,128)S(1)} %collective-permute-done, f32[8,1024,128]{2,1,0:T(8,128)} %param.10, f32[128]{0:T(128)S(1)} %compare_convert_fusion, f32[8,1024]{1,0:T(8,128)S(1)} %bitcast.96), kind=kLoop, calls=%fused_computation.42 | loop fusion | flops 15728640 | bytes 13664768 | tf_op jit(solution)/shard_map/add | solution.py:68
  37.5 1.9 collective-permute-start.2
  39.5 2.4 collective-permute-start.3
  41.9 4.3 %collective-permute-done.2 = f32[1,1,1024,128]{3,2,1,0:T(8,128)S(1)} collective-permute-done((f32[1,1,1024,128]{3,2,1,0:T(8,128)S(1)}, f32[1,1,1024,128]{3,2,1,0:T(8,128)S(1)}, u32[]{:S(2)}, u32[]{:S(2)}) %collective-permute-start.2) | collective-permute-done | bytes 524320 | tf_op jit(solution)/shard_map/ppermute | solution.py:21
  46.1 8.3 %collective-permute-done.3 = f32[1,1,1024,128]{3,2,1,0:T(8,128)S(1)} collective-permute-done((f32[1,1,1024,128]{3,2,1,0:T(8,128)S(1)}, f32[1,1,1024,128]{3,2,1,0:T(8,128)S(1)}, u32[]{:S(2)}, u32[]{:S(2)}) %collective-permute-start.3) | collective-permute-done | bytes 524320 | tf_op jit(solution)/shard_map/ppermute | solution.py:18
  54.5 4.4 %fusion.5 = f32[1,8,1024,128]{3,2,1,0:T(8,128)S(1)} fusion(f32[1,8,1024,128]{3,2,1,0:T(8,128)S(1)} %fusion.2, f32[1,1,1024,128]{3,2,1,0:T(8,128)S(1)} %collective-permute-done.3, f32[1,1,1024,128]{3,2,1,0:T(8,128)S(1)} %collective-permute-done.2, f32[8,1024,128]{2,1,0:T(8,128)S(1)} %copy-done.2, f32[128]{0:T(128)S(1)} %compare_convert_fusion, ...), kind=kLoop, calls=%fused_computation.45 | loop fusion | flops 15728640 | bytes 13664768 | tf_op jit(solution)/shard_map/add | solution.py:68
  59.0 1.9 collective-permute-start.4
  60.9 2.4 collective-permute-start.5
  63.3 4.3 %collective-permute-done.4 = f32[1,1,1024,128]{3,2,1,0:T(8,128)S(1)} collective-permute-done((f32[1,1,1024,128]{3,2,1,0:T(8,128)S(1)}, f32[1,1,1024,128]{3,2,1,0:T(8,128)S(1)}, u32[]{:S(2)}, u32[]{:S(2)}) %collective-permute-start.4) | collective-permute-done | bytes 524320 | tf_op jit(solution)/shard_map/ppermute | solution.py:21
  67.6 8.3 %collective-permute-done.5 = f32[1,1,1024,128]{3,2,1,0:T(8,128)S(1)} collective-permute-done((f32[1,1,1024,128]{3,2,1,0:T(8,128)S(1)}, f32[1,1,1024,128]{3,2,1,0:T(8,128)S(1)}, u32[]{:S(2)}, u32[]{:S(2)}) %collective-permute-start.5) | collective-permute-done | bytes 524320 | tf_op jit(solution)/shard_map/ppermute | solution.py:18
  75.9 4.4 %fusion.8 = f32[1,8,1024,128]{3,2,1,0:T(8,128)S(1)} fusion(f32[1,8,1024,128]{3,2,1,0:T(8,128)S(1)} %fusion.5, f32[1,1,1024,128]{3,2,1,0:T(8,128)S(1)} %collective-permute-done.5, f32[1,1,1024,128]{3,2,1,0:T(8,128)S(1)} %collective-permute-done.4, f32[8,1024,128]{2,1,0:T(8,128)S(1)} %copy-done.2, f32[128]{0:T(128)S(1)} %compare_convert_fusion, ...), kind=kLoop, calls=%fused_computation.48 | loop fusion | flops 15728640 | bytes 13664768 | tf_op jit(solution)/shard_map/add | solution.py:68
  80.4 1.9 collective-permute-start.6
  82.3 2.4 collective-permute-start.7
  84.7 4.3 %collective-permute-done.6 = f32[1,1,1024,128]{3,2,1,0:T(8,128)S(1)} collective-permute-done((f32[1,1,1024,128]{3,2,1,0:T(8,128)S(1)}, f32[1,1,1024,128]{3,2,1,0:T(8,128)S(1)}, u32[]{:S(2)}, u32[]{:S(2)}) %collective-permute-start.6) | collective-permute-done | bytes 524320 | tf_op jit(solution)/shard_map/ppermute | solution.py:21
  89.0 8.3 %collective-permute-done.7 = f32[1,1,1024,128]{3,2,1,0:T(8,128)S(1)} collective-permute-done((f32[1,1,1024,128]{3,2,1,0:T(8,128)S(1)}, f32[1,1,1024,128]{3,2,1,0:T(8,128)S(1)}, u32[]{:S(2)}, u32[]{:S(2)}) %collective-permute-start.7) | collective-permute-done | bytes 524320 | tf_op jit(solution)/shard_map/ppermute | solution.py:18
  97.3 4.4 %fusion.11 = f32[1,8,1024,128]{3,2,1,0:T(8,128)S(1)} fusion(f32[1,8,1024,128]{3,2,1,0:T(8,128)S(1)} %fusion.8, f32[1,1,1024,128]{3,2,1,0:T(8,128)S(1)} %collective-permute-done.7, f32[1,1,1024,128]{3,2,1,0:T(8,128)S(1)} %collective-permute-done.6, f32[8,1024,128]{2,1,0:T(8,128)S(1)} %copy-done.2, f32[128]{0:T(128)S(1)} %compare_convert_fusion, ...), kind=kLoop, calls=%fused_computation.51 | loop fusion | flops 15728640 | bytes 13664768 | tf_op jit(solution)/shard_map/add | solution.py:68
  101.7 1.9 copy-done.4
  105.2 3.7 %all_to_all.25 = f32[2,1,4096]{2,1,0:T(1,128)S(1)} all-to-all(f32[2,1,4096]{2,1,0:T(1,128)S(1)} %reshape.73), channel_id=1, replica_groups=mesh['pat'=2,'gx_0'=4,'gx_1'=2,'gx_2'=4,'gx_3'=2] {'gx_3'}, dimensions={0} | all-to-all | bytes 65536 | tf_op jit(solution)/shard_map/all_to_all | solution.py:41
  111.3 5.9 %all-to-all-start.1 = ((f32[32,1,256]{2,1,0:T(1,128)}), f32[32,1,256]{2,1,0:T(1,128)S(1)}, u32[]{:S(2)}, u32[]{:S(2)}) async-start(f32[32,1,256]{2,1,0:T(1,128)} %reshape.75), calls=%async_computation.1 | async-start | bytes 65536 | tf_op jit(solution)/shard_map/all_to_all | solution.py:41
  118.4 6.2 %collective-permute-start.8 = (f32[1,1,1024,128]{3,2,1,0:T(8,128)S(1)}, f32[1,1,1024,128]{3,2,1,0:T(8,128)S(1)}, u32[]{:S(2)}, u32[]{:S(2)}) collective-permute-start(f32[1,1,1024,128]{3,2,1,0:T(8,128)S(1)} %get-tuple-element.16), channel_id=1, source_target_pairs={{1,0},{2,1},{3,2},{4,3},{5,4},{6,5},{7,6},{8,7},{9,8},{10,9},{11,1... | collective-permute-start | bytes 1572872 | tf_op jit(solution)/shard_map/ppermute | solution.py:21
  124.6 1.9 collective-permute-start.9
  129.9 3.7 %all_to_all.26 = f32[2,1,4096]{2,1,0:T(1,128)S(1)} all-to-all(f32[2,1,4096]{2,1,0:T(1,128)S(1)} %reshape.77), channel_id=1, replica_groups=mesh['pat'=2,'gx_0'=4,'gx_1'=2,'gx_2'=4,'gx_3'=2] {'gx_3'}, dimensions={0} | all-to-all | bytes 65536 | tf_op jit(solution)/shard_map/all_to_all | solution.py:41
  134.8 19.1 %all_to_all.27 = f32[32,1,256]{2,1,0:T(1,128)S(1)} all-to-all(f32[32,1,256]{2,1,0:T(1,128)S(1)} %reshape.79), channel_id=1, replica_groups=mesh['pat'=2,'gx_0'=4,'gx_1'=2,'gx_2'=4,'gx_3'=2] {'gx_0','gx_1','gx_2'}, dimensions={0} | all-to-all | bytes 65536 | tf_op jit(solution)/shard_map/all_to_all | solution.py:41
  155.0 14.4 %fusion.14 = f32[1,8,1024,128]{3,2,1,0:T(8,128)S(1)} fusion(f32[1,8,1024,128]{3,2,1,0:T(8,128)} %param.12, f32[1,1,1024,128]{3,2,1,0:T(8,128)S(1)} %collective-permute-done.9, f32[1,1,1024,128]{3,2,1,0:T(8,128)S(1)} %collective-permute-done.8, f32[8,1024,128]{2,1,0:T(8,128)} %param.10, f32[8,1024]{1,0:T(8,128)S(1)} %mul.172, f32[128]{0:T(128)S(1)} %compare_convert_fusion), kind=kLoop, calls=%fused_computation.54 | loop fusion | flops 15728640 | bytes 13664768 | tf_op jit(solution)/shard_map/add | solution.py:68
  169.4 2.6 collective-permute-start.10
  172.0 1.9 collective-permute-start.11
  173.9 4.7 %collective-permute-done.10 = f32[1,1,1024,128]{3,2,1,0:T(8,128)S(1)} collective-permute-done((f32[1,1,1024,128]{3,2,1,0:T(8,128)S(1)}, f32[1,1,1024,128]{3,2,1,0:T(8,128)S(1)}, u32[]{:S(2)}, u32[]{:S(2)}) %collective-permute-start.10) | collective-permute-done | bytes 524320 | tf_op jit(solution)/shard_map/ppermute | solution.py:21
  178.7 8.3 %collective-permute-done.11 = f32[1,1,1024,128]{3,2,1,0:T(8,128)S(1)} collective-permute-done((f32[1,1,1024,128]{3,2,1,0:T(8,128)S(1)}, f32[1,1,1024,128]{3,2,1,0:T(8,128)S(1)}, u32[]{:S(2)}, u32[]{:S(2)}) %collective-permute-start.11) | collective-permute-done | bytes 524320 | tf_op jit(solution)/shard_map/ppermute | solution.py:18
  187.0 4.4 %fusion.17 = f32[1,8,1024,128]{3,2,1,0:T(8,128)S(1)} fusion(f32[1,8,1024,128]{3,2,1,0:T(8,128)S(1)} %fusion.14, f32[1,1,1024,128]{3,2,1,0:T(8,128)S(1)} %collective-permute-done.11, f32[1,1,1024,128]{3,2,1,0:T(8,128)S(1)} %collective-permute-done.10, f32[8,1024,128]{2,1,0:T(8,128)S(1)} %copy-done.3, f32[8,1024]{1,0:T(8,128)S(1)} %mul.172, ...), kind=kLoop, calls=%fused_computation.57 | loop fusion | flops 15728640 | bytes 13664768 | tf_op jit(solution)/shard_map/add | solution.py:68
  191.5 1.9 collective-permute-start.12
  193.4 2.4 collective-permute-start.13
  195.8 4.3 %collective-permute-done.12 = f32[1,1,1024,128]{3,2,1,0:T(8,128)S(1)} collective-permute-done((f32[1,1,1024,128]{3,2,1,0:T(8,128)S(1)}, f32[1,1,1024,128]{3,2,1,0:T(8,128)S(1)}, u32[]{:S(2)}, u32[]{:S(2)}) %collective-permute-start.12) | collective-permute-done | bytes 524320 | tf_op jit(solution)/shard_map/ppermute | solution.py:21
  200.1 8.3 %collective-permute-done.13 = f32[1,1,1024,128]{3,2,1,0:T(8,128)S(1)} collective-permute-done((f32[1,1,1024,128]{3,2,1,0:T(8,128)S(1)}, f32[1,1,1024,128]{3,2,1,0:T(8,128)S(1)}, u32[]{:S(2)}, u32[]{:S(2)}) %collective-permute-start.13) | collective-permute-done | bytes 524320 | tf_op jit(solution)/shard_map/ppermute | solution.py:18
  208.4 4.4 %fusion.20 = f32[1,8,1024,128]{3,2,1,0:T(8,128)S(1)} fusion(f32[1,8,1024,128]{3,2,1,0:T(8,128)S(1)} %fusion.17, f32[1,1,1024,128]{3,2,1,0:T(8,128)S(1)} %collective-permute-done.13, f32[1,1,1024,128]{3,2,1,0:T(8,128)S(1)} %collective-permute-done.12, f32[8,1024,128]{2,1,0:T(8,128)S(1)} %copy-done.3, f32[8,1024]{1,0:T(8,128)S(1)} %mul.172, ...), kind=kLoop, calls=%fused_computation.60 | loop fusion | flops 15728640 | bytes 13664768 | tf_op jit(solution)/shard_map/add | solution.py:68
  212.9 1.9 collective-permute-start.14
  214.8 2.4 collective-permute-start.15
  217.3 4.3 %collective-permute-done.14 = f32[1,1,1024,128]{3,2,1,0:T(8,128)S(1)} collective-permute-done((f32[1,1,1024,128]{3,2,1,0:T(8,128)S(1)}, f32[1,1,1024,128]{3,2,1,0:T(8,128)S(1)}, u32[]{:S(2)}, u32[]{:S(2)}) %collective-permute-start.14) | collective-permute-done | bytes 524320 | tf_op jit(solution)/shard_map/ppermute | solution.py:21
  221.5 8.3 %collective-permute-done.15 = f32[1,1,1024,128]{3,2,1,0:T(8,128)S(1)} collective-permute-done((f32[1,1,1024,128]{3,2,1,0:T(8,128)S(1)}, f32[1,1,1024,128]{3,2,1,0:T(8,128)S(1)}, u32[]{:S(2)}, u32[]{:S(2)}) %collective-permute-start.15) | collective-permute-done | bytes 524320 | tf_op jit(solution)/shard_map/ppermute | solution.py:18
  229.9 4.8 %fusion.25 = f32[1,8,1024,128]{3,2,1,0:T(8,128)S(1)} fusion(f32[1,8,1024,128]{3,2,1,0:T(8,128)S(1)} %copy-done.5, f32[1,8,1024,128]{3,2,1,0:T(8,128)S(1)} %fusion.20, f32[1,1,1024,128]{3,2,1,0:T(8,128)S(1)} %collective-permute-done.15, f32[1,1,1024,128]{3,2,1,0:T(8,128)S(1)} %collective-permute-done.14, f32[8,1024,128]{2,1,0:T(8,128)S(1)} %copy-done.3, ...), kind=kLoop, calls=%fused_computation.65 | loop fusion | flops 17825792 | bytes 17859072 | tf_op jit(solution)/shard_map/neg | solution.py:110
  234.6 2.3 copy.32
  236.9 5.6 %all-to-all-start.4 = ((f32[2,8,512,128]{3,2,1,0:T(8,128)}), f32[2,8,512,128]{3,2,1,0:T(8,128)}, u32[]{:S(2)}, u32[]{:S(2)}) async-start(f32[2,8,512,128]{3,2,1,0:T(8,128)} %copy.32), calls=%async_computation.4 | async-start | bytes 8388608 | tf_op jit(solution)/shard_map/all_to_all | solution.py:53
  243.2 40.7 %all-to-all-done.4 = f32[2,8,512,128]{3,2,1,0:T(8,128)} async-done(((f32[2,8,512,128]{3,2,1,0:T(8,128)}), f32[2,8,512,128]{3,2,1,0:T(8,128)}, u32[]{:S(2)}, u32[]{:S(2)}) %all-to-all-start.4) | async-done | bytes 4194336 | tf_op jit(solution)/shard_map/all_to_all | solution.py:53
  283.9 4.0 %reduce_sum.8 = f32[8,512,128]{2,1,0:T(8,128)} reduce(f32[2,8,512,128]{3,2,1,0:T(8,128)} %all-to-all-done.4, f32[]{:T(128)} %constant.13.clone.1), dimensions={0}, to_apply=%region_0.1 | reduce | flops 524288 | bytes 6291460 | tf_op jit(solution)/shard_map/reduce_sum | solution.py:54
  (57 shorter events, 12.1 us)
Async XLA Ops:
  0.6 10.3 %copy-start = (f32[8,8,1024]{2,1,0:T(8,128)S(1)}, f32[8,8,1024]{2,1,0:T(8,128)}, u32[]{:S(2)}) copy-start(f32[8,8,1024]{2,1,0:T(8,128)} %param.8) | copy-start | bytes 786436
  2.0 13.1 %collective-permute-start = (f32[1,1,1024,128]{3,2,1,0:T(8,128)S(1)}, f32[1,1,1024,128]{3,2,1,0:T(8,128)S(1)}, u32[]{:S(2)}, u32[]{:S(2)}) collective-permute-start(f32[1,1,1024,128]{3,2,1,0:T(8,128)S(1)} %get-tuple-element.24), channel_id=1, source_target_pairs={{1,0},{2,1},{3,2},{4,3},{5,4},{6,5},{7,6},{8,7},{9,8},{10,9},{11,1... | collective-permute-start | bytes 1572872 | tf_op jit(solution)/shard_map/ppermute | solution.py:21
  8.3 15.0 %collective-permute-start.1 = (f32[1,1,1024,128]{3,2,1,0:T(8,128)S(1)}, f32[1,1,1024,128]{3,2,1,0:T(8,128)S(1)}, u32[]{:S(2)}, u32[]{:S(2)}) collective-permute-start(f32[1,1,1024,128]{3,2,1,0:T(8,128)S(1)} %get-tuple-element.25), channel_id=1, source_target_pairs={{0,1},{1,2},{2,3},{3,4},{4,5},{5,6},{6,7},{7,8},{8,9},{9,10},{10,1... | collective-permute-start | bytes 1572872 | tf_op jit(solution)/shard_map/ppermute | solution.py:18
  23.3 31.1 %copy-start.2 = (f32[8,1024,128]{2,1,0:T(8,128)S(1)}, f32[8,1024,128]{2,1,0:T(8,128)}, u32[]{:S(2)}) copy-start(f32[8,1024,128]{2,1,0:T(8,128)} %param.10) | copy-start | bytes 12582916
  37.5 8.6 %collective-permute-start.2 = (f32[1,1,1024,128]{3,2,1,0:T(8,128)S(1)}, f32[1,1,1024,128]{3,2,1,0:T(8,128)S(1)}, u32[]{:S(2)}, u32[]{:S(2)}) collective-permute-start(f32[1,1,1024,128]{3,2,1,0:T(8,128)S(1)} %get-tuple-element.22), channel_id=1, source_target_pairs={{1,0},{2,1},{3,2},{4,3},{5,4},{6,5},{7,6},{8,7},{9,8},{10,9},{11,1... | collective-permute-start | bytes 1572872 | tf_op jit(solution)/shard_map/ppermute | solution.py:21
  39.5 15.0 %collective-permute-start.3 = (f32[1,1,1024,128]{3,2,1,0:T(8,128)S(1)}, f32[1,1,1024,128]{3,2,1,0:T(8,128)S(1)}, u32[]{:S(2)}, u32[]{:S(2)}) collective-permute-start(f32[1,1,1024,128]{3,2,1,0:T(8,128)S(1)} %get-tuple-element.23), channel_id=1, source_target_pairs={{0,1},{1,2},{2,3},{3,4},{4,5},{5,6},{6,7},{7,8},{8,9},{9,10},{10,1... | collective-permute-start | bytes 1572872 | tf_op jit(solution)/shard_map/ppermute | solution.py:18
  59.0 8.6 %collective-permute-start.4 = (f32[1,1,1024,128]{3,2,1,0:T(8,128)S(1)}, f32[1,1,1024,128]{3,2,1,0:T(8,128)S(1)}, u32[]{:S(2)}, u32[]{:S(2)}) collective-permute-start(f32[1,1,1024,128]{3,2,1,0:T(8,128)S(1)} %get-tuple-element.20), channel_id=1, source_target_pairs={{1,0},{2,1},{3,2},{4,3},{5,4},{6,5},{7,6},{8,7},{9,8},{10,9},{11,1... | collective-permute-start | bytes 1572872 | tf_op jit(solution)/shard_map/ppermute | solution.py:21
  60.9 15.0 %collective-permute-start.5 = (f32[1,1,1024,128]{3,2,1,0:T(8,128)S(1)}, f32[1,1,1024,128]{3,2,1,0:T(8,128)S(1)}, u32[]{:S(2)}, u32[]{:S(2)}) collective-permute-start(f32[1,1,1024,128]{3,2,1,0:T(8,128)S(1)} %get-tuple-element.21), channel_id=1, source_target_pairs={{0,1},{1,2},{2,3},{3,4},{4,5},{5,6},{6,7},{7,8},{8,9},{9,10},{10,1... | collective-permute-start | bytes 1572872 | tf_op jit(solution)/shard_map/ppermute | solution.py:18
  80.4 8.6 %collective-permute-start.6 = (f32[1,1,1024,128]{3,2,1,0:T(8,128)S(1)}, f32[1,1,1024,128]{3,2,1,0:T(8,128)S(1)}, u32[]{:S(2)}, u32[]{:S(2)}) collective-permute-start(f32[1,1,1024,128]{3,2,1,0:T(8,128)S(1)} %get-tuple-element.18), channel_id=1, source_target_pairs={{1,0},{2,1},{3,2},{4,3},{5,4},{6,5},{7,6},{8,7},{9,8},{10,9},{11,1... | collective-permute-start | bytes 1572872 | tf_op jit(solution)/shard_map/ppermute | solution.py:21
  82.3 15.0 %collective-permute-start.7 = (f32[1,1,1024,128]{3,2,1,0:T(8,128)S(1)}, f32[1,1,1024,128]{3,2,1,0:T(8,128)S(1)}, u32[]{:S(2)}, u32[]{:S(2)}) collective-permute-start(f32[1,1,1024,128]{3,2,1,0:T(8,128)S(1)} %get-tuple-element.19), channel_id=1, source_target_pairs={{0,1},{1,2},{2,3},{3,4},{4,5},{5,6},{6,7},{7,8},{8,9},{9,10},{10,1... | collective-permute-start | bytes 1572872 | tf_op jit(solution)/shard_map/ppermute | solution.py:18
  101.7 2.0 copy-start.4
  103.7 22.9 %copy-start.6 = (f32[1,2,16,16]{3,2,1,0:T(8,128)S(1)}, f32[1,2,16,16]{3,2,1,0:T(8,128)}, u32[]{:S(2)}) copy-start(f32[1,2,16,16]{3,2,1,0:T(8,128)} %param.13) | copy-start | bytes 6148
  103.7 23.8 %copy-start.7 = (s32[16]{0:T(128)S(1)}, s32[16]{0:T(128)}, u32[]{:S(2)}) copy-start(s32[16]{0:T(128)} %param.9) | copy-start | bytes 196
  111.3 15.4 %all-to-all-start.1 = ((f32[32,1,256]{2,1,0:T(1,128)}), f32[32,1,256]{2,1,0:T(1,128)S(1)}, u32[]{:S(2)}, u32[]{:S(2)}) async-start(f32[32,1,256]{2,1,0:T(1,128)} %reshape.75), calls=%async_computation.1 | async-start | bytes 65536 | tf_op jit(solution)/shard_map/all_to_all | solution.py:41
  118.4 36.5 %collective-permute-start.8 = (f32[1,1,1024,128]{3,2,1,0:T(8,128)S(1)}, f32[1,1,1024,128]{3,2,1,0:T(8,128)S(1)}, u32[]{:S(2)}, u32[]{:S(2)}) collective-permute-start(f32[1,1,1024,128]{3,2,1,0:T(8,128)S(1)} %get-tuple-element.16), channel_id=1, source_target_pairs={{1,0},{2,1},{3,2},{4,3},{5,4},{6,5},{7,6},{8,7},{9,8},{10,9},{11,1... | collective-permute-start | bytes 1572872 | tf_op jit(solution)/shard_map/ppermute | solution.py:21
  124.6 30.3 %collective-permute-start.9 = (f32[1,1,1024,128]{3,2,1,0:T(8,128)S(1)}, f32[1,1,1024,128]{3,2,1,0:T(8,128)S(1)}, u32[]{:S(2)}, u32[]{:S(2)}) collective-permute-start(f32[1,1,1024,128]{3,2,1,0:T(8,128)S(1)} %get-tuple-element.17), channel_id=1, source_target_pairs={{0,1},{1,2},{2,3},{3,4},{4,5},{5,6},{6,7},{7,8},{8,9},{9,10},{10,1... | collective-permute-start | bytes 1572872 | tf_op jit(solution)/shard_map/ppermute | solution.py:18
  155.0 32.1 %copy-start.3 = (f32[8,1024,128]{2,1,0:T(8,128)S(1)}, f32[8,1024,128]{2,1,0:T(8,128)}, u32[]{:S(2)}) copy-start(f32[8,1024,128]{2,1,0:T(8,128)} %param.10) | copy-start | bytes 12582916
  169.4 9.3 %collective-permute-start.10 = (f32[1,1,1024,128]{3,2,1,0:T(8,128)S(1)}, f32[1,1,1024,128]{3,2,1,0:T(8,128)S(1)}, u32[]{:S(2)}, u32[]{:S(2)}) collective-permute-start(f32[1,1,1024,128]{3,2,1,0:T(8,128)S(1)} %get-tuple-element.14), channel_id=1, source_target_pairs={{1,0},{2,1},{3,2},{4,3},{5,4},{6,5},{7,6},{8,7},{9,8},{10,9},{11,1... | collective-permute-start | bytes 1572872 | tf_op jit(solution)/shard_map/ppermute | solution.py:21
  172.0 15.0 %collective-permute-start.11 = (f32[1,1,1024,128]{3,2,1,0:T(8,128)S(1)}, f32[1,1,1024,128]{3,2,1,0:T(8,128)S(1)}, u32[]{:S(2)}, u32[]{:S(2)}) collective-permute-start(f32[1,1,1024,128]{3,2,1,0:T(8,128)S(1)} %get-tuple-element.15), channel_id=1, source_target_pairs={{0,1},{1,2},{2,3},{3,4},{4,5},{5,6},{6,7},{7,8},{8,9},{9,10},{10,1... | collective-permute-start | bytes 1572872 | tf_op jit(solution)/shard_map/ppermute | solution.py:18
  191.5 8.6 %collective-permute-start.12 = (f32[1,1,1024,128]{3,2,1,0:T(8,128)S(1)}, f32[1,1,1024,128]{3,2,1,0:T(8,128)S(1)}, u32[]{:S(2)}, u32[]{:S(2)}) collective-permute-start(f32[1,1,1024,128]{3,2,1,0:T(8,128)S(1)} %get-tuple-element.12), channel_id=1, source_target_pairs={{1,0},{2,1},{3,2},{4,3},{5,4},{6,5},{7,6},{8,7},{9,8},{10,9},{11,1... | collective-permute-start | bytes 1572872 | tf_op jit(solution)/shard_map/ppermute | solution.py:21
  193.4 15.0 %collective-permute-start.13 = (f32[1,1,1024,128]{3,2,1,0:T(8,128)S(1)}, f32[1,1,1024,128]{3,2,1,0:T(8,128)S(1)}, u32[]{:S(2)}, u32[]{:S(2)}) collective-permute-start(f32[1,1,1024,128]{3,2,1,0:T(8,128)S(1)} %get-tuple-element.13), channel_id=1, source_target_pairs={{0,1},{1,2},{2,3},{3,4},{4,5},{5,6},{6,7},{7,8},{8,9},{9,10},{10,1... | collective-permute-start | bytes 1572872 | tf_op jit(solution)/shard_map/ppermute | solution.py:18
  208.4 21.4 %copy-start.5 = (f32[1,8,1024,128]{3,2,1,0:T(8,128)S(1)}, f32[1,8,1024,128]{3,2,1,0:T(8,128)}, u32[]{:S(2)}) copy-start(f32[1,8,1024,128]{3,2,1,0:T(8,128)} %copy-done.4) | copy-start | bytes 12582916
  212.9 8.6 %collective-permute-start.14 = (f32[1,1,1024,128]{3,2,1,0:T(8,128)S(1)}, f32[1,1,1024,128]{3,2,1,0:T(8,128)S(1)}, u32[]{:S(2)}, u32[]{:S(2)}) collective-permute-start(f32[1,1,1024,128]{3,2,1,0:T(8,128)S(1)} %get-tuple-element.10), channel_id=1, source_target_pairs={{1,0},{2,1},{3,2},{4,3},{5,4},{6,5},{7,6},{8,7},{9,8},{10,9},{11,1... | collective-permute-start | bytes 1572872 | tf_op jit(solution)/shard_map/ppermute | solution.py:21
  214.8 15.0 %collective-permute-start.15 = (f32[1,1,1024,128]{3,2,1,0:T(8,128)S(1)}, f32[1,1,1024,128]{3,2,1,0:T(8,128)S(1)}, u32[]{:S(2)}, u32[]{:S(2)}) collective-permute-start(f32[1,1,1024,128]{3,2,1,0:T(8,128)S(1)} %get-tuple-element.11), channel_id=1, source_target_pairs={{0,1},{1,2},{2,3},{3,4},{4,5},{5,6},{6,7},{7,8},{8,9},{9,10},{10,1... | collective-permute-start | bytes 1572872 | tf_op jit(solution)/shard_map/ppermute | solution.py:18
  236.9 47.0 %all-to-all-start.4 = ((f32[2,8,512,128]{3,2,1,0:T(8,128)}), f32[2,8,512,128]{3,2,1,0:T(8,128)}, u32[]{:S(2)}, u32[]{:S(2)}) async-start(f32[2,8,512,128]{3,2,1,0:T(8,128)} %copy.32), calls=%async_computation.4 | async-start | bytes 8388608 | tf_op jit(solution)/shard_map/all_to_all | solution.py:53
  242.5 45.3 %copy-start.1 = (f32[8,8,1024]{2,1,0:T(8,128)S(1)}, f32[8,8,1024]{2,1,0:T(8,128)}, u32[]{:S(2)}) copy-start(f32[8,8,1024]{2,1,0:T(8,128)} %param.8) | copy-start | bytes 786436
where the time goes:
time: 289 us; the launch traced here: 288 us
  waiting for transfers between devices  129 us (45%)
  other arithmetic  62.1 us (21%)
  starting transfers between devices  54 us (19%)
  blocking collectives  26.6 us (9%)
  local copies, waits for them, and re-layouts  12.4 us (4%)
    ppermute x8, waiting for transfers between devices, extended(): lax.ppermute(lax.slice_in_dim(block, block.shape[dim] - width, None, axis...  58.3 us
    add x7, other arithmetic, relax_step(): return inner + weight * drive / diag  50.4 us
    all_to_all x1, waiting for transfers between devices, sum_at_owner(): lax.all_to_all(pieces, axis, split_axis=0, concat_axis=0, tiled=True)  40.7 us
    ppermute x8, waiting for transfers between devices, extended(): lax.ppermute(lax.slice_in_dim(block, 0, width, axis=dim), axis, backward)  29.7 us
    all_to_all x3, blocking collectives, moved_by_axis(): filled = lax.all_to_all(filled, axes[k], k, k, tiled=True)  26.6 us
    ppermute x8, starting transfers between devices, extended(): lax.ppermute(lax.slice_in_dim(block, 0, width, axis=dim), axis, backward)  24.7 us
    ppermute x8, starting transfers between devices, extended(): lax.ppermute(lax.slice_in_dim(block, block.shape[dim] - width, None, axis...  17.8 us
    all_to_all x1, starting transfers between devices, moved_by_axis(): filled = lax.all_to_all(filled, axes[k], k, k, tiled=True)  5.87 us
  transfers between devices with their start and end apart: 18, of which 15 were waited for; matrix products, arithmetic and copies ran while one was open for 3% of the time, Pallas kernels for 0%

commit v1 on v0

v1 whole, which is shorter than its diff:
```python
import functools
import math

import jax
import jax.numpy as jnp
from jax import lax
from jax.experimental import pallas as pl
from jax.experimental.pallas import tpu as pltpu
from jax.sharding import Mesh
from jax.sharding import PartitionSpec as P

SWEEPS = 4
GX = ("gx_0", "gx_1", "gx_2", "gx_3")
ALL = ("pat",) + GX
CHUNKS = ((True, 0, 256), (True, 256, 256), (False, 0, 512))
HIGH = lax.Precision.HIGHEST
F32 = jnp.float32


def sweep_weight(sweep):
    return 1.0 / (1.25 + 0.75 * math.cos(math.pi * (2 * sweep + 1) / (2 * SWEEPS)))


def halo_rows(rows, ny):
    return rows + 8 if 2 * rows == ny else rows + 16


def chunk_start(meta_ref, sends, offset, half):
    pat = meta_ref[0]
    which = 1 - pat if sends else pat
    return which * half + offset


def iota(shape, dim):
    return lax.broadcasted_iota(jnp.int32, shape, dim)


def face_copies(meta, bufs, base, near, far, sem, chunk, ny):
    sends, offset, rows = chunk
    nh = halo_rows(rows, ny)
    y0 = chunk_start(meta, sends, offset, ny // 2)
    s = pl.multiple_of(jnp.clip(y0 - 8, 0, ny - nh) - base, 8)
    core = meta[4]
    outs = []
    for k, (arr, at, count) in enumerate(zip(bufs, (0, 4, 8), (4, 4, 3))):
        top = 8 - count
        for i, (dst, x) in enumerate(((far, core * top), (near, (1 - core) * top))):
            cp = pltpu.make_async_copy(
                arr.at[pl.ds(x, count), pl.ds(s, nh), :], dst.at[pl.ds(at, count)], sem.at[i, k]
            )
            cp.start()
            outs.append(cp)
    return outs


def faces_kernel(meta, fwd, adj, absn, near, far, fs, ad, ab, in_sem, sem, *, chunk, ny):
    sends, offset, rows = chunk
    nh = halo_rows(rows, ny)
    y0 = chunk_start(meta, sends, offset, ny // 2)
    s = pl.multiple_of(jnp.clip(y0 - 8, 0, ny - nh), 8)
    loads = []
    for i, (h, v) in enumerate(((fwd, fs), (adj, ad), (absn, ab))):
        cp = pltpu.make_async_copy(h.at[:, pl.ds(s, nh), :], v, in_sem.at[i])
        cp.start()
        loads.append(cp)
    for cp in loads:
        cp.wait()
    for cp in face_copies(meta, (fs, ad, ab), s, near, far, sem, chunk, ny):
        cp.wait()


def faces_call(meta, fwd, adj, absn, chunk):
    ny = fwd.shape[1]
    nh = halo_rows(chunk[2], ny)
    any_spec = pl.BlockSpec(memory_space=pl.ANY)
    return pl.pallas_call(
        functools.partial(faces_kernel, chunk=chunk, ny=ny),
        out_shape=[jax.ShapeDtypeStruct((11, nh, 128), F32)] * 2,
        in_specs=[pl.BlockSpec(memory_space=pltpu.SMEM)] + [any_spec] * 3,
        out_specs=[any_spec] * 2,
        scratch_shapes=[pltpu.VMEM((8, nh, 128), F32)] * 3
        + [pltpu.SemaphoreType.DMA((3,)), pltpu.SemaphoreType.DMA((2, 3))],
        name="faces",
    )(meta, fwd, adj, absn)


def pack_kernel(meta, fwd, adj, absn, pats, *rest, chunks, ny):
    n = 2 * len(chunks)
    faces = rest[:n]
    t1, t2, src, near, far, fs, ad, ab, p1, p2, in_sem, src_sem, face_sem = rest[n:]
    loads = []
    for i, (h, v) in enumerate(((fwd, fs), (adj, ad), (absn, ab))):
        cp = pltpu.make_async_copy(h, v, in_sem.at[i])
        cp.start()
        loads.append(cp)
    src_cp = pltpu.make_async_copy(pats.at[meta[3]], src, src_sem)
    src_cp.start()
    lane = iota((8, 128), 1)
    un = 8

    def pack(parts, dst):
        def body(t, carry):
            done = []
            for u in range(un):
                y = pl.multiple_of((t * un + u) * 8, 8)
                acc = jnp.zeros((8, 128), F32)
                for arr, base in parts:
                    for x in range(8):
                        at = base + 8 * x
                        v = arr[x, pl.ds(y, 8), :]
                        v = pltpu.roll(v, at, axis=1) if at else v
                        acc = jnp.where((lane >= at) & (lane < at + 8), v, acc)
                done.append((y, acc))
            for y, acc in done:
                dst[pl.ds(y, 8), :] = acc
            return carry

        lax.fori_loop(0, ny // (8 * un), body, 0)

    for cp in loads:
        cp.wait()
    outs = []
    for c, chunk in enumerate(chunks):
        outs += face_copies(
            meta, (fs, ad, ab), 0, faces[2 * c], faces[2 * c + 1], face_sem.at[c], chunk, ny
        )
    pack(((fs, 0), (ad, 64)), p1)
    pack(((ab, 0),), p2)
    for v in range(ny // 128):
        t1[:, v * 128 : (v + 1) * 128] = p1[v * 128 : (v + 1) * 128, :].T
        t2[:, v * 128 : (v + 1) * 128] = p2[v * 128 : (v + 1) * 128, :].T[:64]
    src_cp.wait()

    def high_face(dst):
        dst[0:32, :] = t1[32:64, :]
        dst[32:64, :] = t1[96:128, :]
        dst[64:88, :] = t2[40:64, :]
        dst[88:96, :] = pltpu.roll(src[...], 3, axis=0)

    def low_face(dst):
        dst[0:32, :] = t1[0:32, :]
        dst[32:64, :] = t1[64:96, :]
        dst[64:88, :] = t2[0:24, :]
        dst[88:96, :] = src[...]

    @pl.when(meta[4] == 0)
    def _():
        high_face(near)
        low_face(far)

    @pl.when(meta[4] != 0)
    def _():
        low_face(near)
        high_face(far)

    for cp in outs:
        cp.wait()


def pack_call(meta, fwd, adj, absn, pats, chunks):
    ny = fwd.shape[1]
    small = [(128, ny), (64, ny), (8, ny), (96, ny), (96, ny)]
    shapes = []
    for _, _, rows in chunks:
        shapes += [(11, halo_rows(rows, ny), 128)] * 2
    any_spec = pl.BlockSpec(memory_space=pl.ANY)
    vmem = pl.BlockSpec(memory_space=pltpu.VMEM)
    return pl.pallas_call(
        functools.partial(pack_kernel, chunks=chunks, ny=ny),
        out_shape=[jax.ShapeDtypeStruct(s, F32) for s in shapes + small],
        in_specs=[pl.BlockSpec(memory_space=pltpu.SMEM)] + [any_spec] * 4,
        out_specs=[any_spec] * len(shapes) + [vmem] * 5,
        scratch_shapes=[pltpu.VMEM((8, ny, 128), F32)] * 3
        + [pltpu.VMEM((ny, 128), F32)] * 2
        + [
            pltpu.SemaphoreType.DMA((3,)),
            pltpu.SemaphoreType.DMA(()),
            pltpu.SemaphoreType.DMA((len(chunks), 2, 3)),
        ],
        name="pack",
    )(meta, fwd, adj, absn, pats)


def group_transpose(v):
    row = iota((8, 128), 0)
    group = iota((8, 128), 1) // 16
    for b in (1, 2, 4):
        rb = (row // b) % 2
        gb = (group // b) % 2
        down = pltpu.roll(pltpu.roll(v, b, axis=0), 128 - 16 * b, axis=1)
        upw = pltpu.roll(pltpu.roll(v, 8 - b, axis=0), 16 * b, axis=1)
        v = jnp.where(rb == gb, v, jnp.where(rb == 1, down, upw))
    return v


def shallow_solve(meta, start, at, near, far, near_at, t2, f0, f1, r, s, ny):
    lo_ok = jnp.where(meta[1] > 0, 1.0, 0.0).astype(F32)
    hi_ok = jnp.where(meta[2] > 0, 1.0, 0.0).astype(F32)
    core0 = meta[4] == 0

    def side(row):
        a = near[row : row + 8, :]
        b = far[row : row + 8, :]
        return jnp.where(core0, b, a), jnp.where(core0, a, b)

    for i in range(4):
        f0[i], f0[12 + i] = side(near_at + 8 * i)
    for i in range(8):
        f0[4 + i] = start[at + 8 * i : at + 8 * i + 8, :]
        r[4 + i] = 1.0 / (6.0 + t2[8 * i : 8 * i + 8, :])
    for i in range(3):
        lo, hi = side(64 + 8 * i)
        r[1 + i] = lo_ok / (6.0 + lo)
        r[12 + i] = hi_ok / (6.0 + hi)
    zi = iota((8, ny), 0)
    yi = iota((8, ny), 1)
    bufs = (f0, f1)
    for k in range(SWEEPS):
        w = sweep_weight(k)
        old, new = bufs[k % 2], bufs[1 - k % 2]

        def pair(q, carry, old=old, new=new, w=w, k=k):
            p = k + 1 + 2 * q
            v = [old[p - 1 + i] for i in range(4)]
            for i in range(2):
                c = v[i + 1]
                nb = v[i] + v[i + 2]
                nb = nb + jnp.where(yi == 0, 0.0, pltpu.roll(c, 1, axis=1))
                nb = nb + jnp.where(yi == ny - 1, 0.0, pltpu.roll(c, ny - 1, axis=1))
                nb = nb + jnp.where(zi == 0, 0.0, pltpu.roll(c, 1, axis=0))
                nb = nb + jnp.where(zi == 7, 0.0, pltpu.roll(c, 7, axis=0))
                new[p + i] = (1.0 - w) * c + (w * r[p + i]) * (nb + s[p + i])
            return carry

        lax.fori_loop(0, 7 - k, pair, 0)


def forward_kernel(meta, t1, t2, src, near, far, fsh, surf, f0, f1, r, s, *, ny):
    z0 = iota((8, ny), 0) == 0
    core0 = meta[4] == 0
    for i in range(3):
        a = near[88 + i : 89 + i, :]
        b = far[88 + i : 89 + i, :]
        s[1 + i] = jnp.where(z0, jnp.where(core0, b, a), 0.0)
        s[12 + i] = jnp.where(z0, jnp.where(core0, a, b), 0.0)
    for i in range(8):
        s[4 + i] = jnp.where(z0, src[i : i + 1, :], 0.0)
    shallow_solve(meta, t1, 0, near, far, 0, t2, f0, f1, r, s, ny)
    for i in range(8):
        fsh[i] = f0[4 + i]
    top = jnp.concatenate([f0[4 + i, 0:1, :] for i in range(8)], axis=0)
    for v in range(ny // 128):
        surf[8 * v : 8 * v + 8, :] = group_transpose(top[:, 128 * v : 128 * v + 128])


def shallow_scratch(ny):
    return [pltpu.VMEM((16, 8, ny), F32)] * 4


def vmem_call(kernel, out_shapes, scratch, n_in):
    vmem = pl.BlockSpec(memory_space=pltpu.VMEM)
    return pl.pallas_call(
        kernel,
        out_shape=[jax.ShapeDtypeStruct(s, F32) for s in out_shapes],
        in_specs=[pl.BlockSpec(memory_space=pltpu.SMEM)] + [vmem] * n_in,
        out_specs=[vmem] * len(out_shapes),
        scratch_shapes=scratch,
    )


def adjoint_kernel(
    meta, t1, t2, got, near, far, fsh, send, keep, f0, f1, r, s, prod, *, ny
):
    z0 = iota((8, ny), 0) == 0
    for h in range(2):
        parts = []
        for v in range(ny // 128):
            parts.append(group_transpose(got[8 * v : 8 * v + 8, 128 * h : 128 * h + 128]))
        rows = jnp.concatenate(parts, axis=1)
        for j in range(8):
            s[8 * h + j] = jnp.where(z0, rows[j : j + 1, :], 0.0)
    shallow_solve(meta, t1, 64, near, far, 32, t2, f0, f1, r, s, ny)
    for i in range(8):
        prod[8 * i : 8 * i + 8, :] = -(fsh[i] * f0[4 + i])
    half = ny // 2

    @pl.when(meta[0] == 0)
    def _():
        keep[...] = prod[:, :half]
        send[...] = prod[:, half:]

    @pl.when(meta[0] != 0)
    def _():
        keep[...] = prod[:, half:]
        send[...] = prod[:, :half]


def data_kernel(meta, got, table, back, measured, model, send):
    lane_group = iota((32, 128), 1) // 16
    full = jnp.dot(table[...], got[...], precision=HIGH, preferred_element_type=F32)
    acc = jnp.zeros((32, 128), F32)
    for x in range(8):
        acc = acc + jnp.where(lane_group == x, full[32 * x : 32 * x + 32, :], 0.0)
    for shift in (64, 32, 16):
        acc = acc + pltpu.roll(acc, shift, axis=1)
    model[...] = acc
    misfit = acc - measured[...]
    rows = lax.dot_general(
        back[...], misfit, (((0,), (0,)), ((), ())), precision=HIGH, preferred_element_type=F32
    )
    count = rows.shape[0] // 16
    group = iota((count, 128), 1) // 16
    for h in range(2):
        out = jnp.zeros((count, 128), F32)
        for j in range(8):
            at = (8 * h + j) * count
            out = jnp.where(group == j, rows[at : at + count, :], out)
        send[:, 128 * h : 128 * h + 128] = out


def tile_count(tiles, most=66):
    return max(u for u in range(1, most + 1) if tiles % u == 0)


def deep_kernel(
    meta, fwd, adj, absn, near, far, out, f0, f1, a0, a1, rb, sem, *, sends, offset, rows, ny
):
    nh = halo_rows(rows, ny)
    y0 = chunk_start(meta, sends, offset, ny // 2)
    s = pl.multiple_of(jnp.clip(y0 - 8, 0, ny - nh), 8)
    off = pl.multiple_of(s - y0 + 16, 8)
    core = meta[4]

    def group(arr, at, count, buf, k):
        below = 4 - count
        cps = [
            pltpu.make_async_copy(
                arr.at[:, pl.ds(s, nh), :], buf.at[pl.ds(4, 8), pl.ds(off, nh), :], sem.at[k, 0]
            ),
            pltpu.make_async_copy(
                near.at[pl.ds(at, count)],
                buf.at[pl.ds(jnp.where(core == 0, 12, below), count), pl.ds(off, nh), :],
                sem.at[k, 1],
            ),
            pltpu.make_async_copy(
                far.at[pl.ds(at, count)],
                buf.at[pl.ds(jnp.where(core == 0, below, 12), count), pl.ds(off, nh), :],
                sem.at[k, 2],
            ),
        ]
        for cp in cps:
            cp.start()
        return cps

    r_cps = group(absn, 8, 3, rb, 0)
    f_cps = group(fwd, 0, 4, f0, 1)
    a_cps = group(adj, 4, 4, a0, 2)
    zero = jnp.zeros((16, 8, 128), F32)

    def edges(buf):
        @pl.when(y0 == 0)
        def _():
            buf[:, 8:16, :] = zero

        @pl.when(y0 + rows == ny)
        def _():
            buf[:, rows + 16 : rows + 24, :] = zero

    edges(f0)
    edges(a0)
    tiles = (rows + 16) // 8
    for cp in r_cps:
        cp.wait()

    def invert(p, carry):
        ok = jnp.where(p < 4, meta[1], jnp.where(p >= 12, meta[2], 1))
        ok = jnp.where(ok > 0, 1.0, 0.0).astype(F32)
        un = tile_count(tiles)

        def block(t, c):
            ys = [pl.multiple_of(8 + (t * un + u) * 8, 8) for u in range(un)]
            new = [ok / (6.0 + rb[p, pl.ds(y, 8), :]) for y in ys]
            for y, v in zip(ys, new):
                rb[p, pl.ds(y, 8), :] = v
            return c

        return lax.fori_loop(0, tiles // un, block, carry)

    lax.fori_loop(1, 15, invert, 0)
    edges(rb)
    last = iota((8, 128), 1) == 127

    def sweep(buf, k, begin, count, store):
        w = sweep_weight(k)
        un = tile_count(count)

        def pair(q, carry):
            p = k + 1 + 2 * q

            def block(t, cc):
                for u in range(un):
                    y = pl.multiple_of(begin + (t * un + u) * 8, 8)
                    v = [buf[p - 1 + i, pl.ds(y, 8), :] for i in range(4)]
                    for i in range(2):
                        c = v[i + 1]
                        ym = buf[p + i, pl.ds(y - 1, 8), :]
                        yp = buf[p + i, pl.ds(y + 1, 8), :]
                        zl = pltpu.roll(c, 1, axis=1)
                        zr = jnp.where(last, 0.0, pltpu.roll(c, 127, axis=1))
                        nb = ((v[i] + v[i + 2]) + (ym + yp)) + (zl + zr)
                        new = ((1.0 - w) / w) * c + rb[p + i, pl.ds(y, 8), :] * nb
                        store(p + i, y, new)
                return cc

            return lax.fori_loop(0, count // un, block, carry)

        lax.fori_loop(0, 7 - k, pair, 0)

    def into(buf):
        def store(p, y, new):
            buf[p, pl.ds(y, 8), :] = new

        return store

    scale = -math.prod(sweep_weight(k) for k in range(SWEEPS)) ** 2

    def product(p, y, new):
        at = pl.multiple_of(y - 16, 8)
        out[p - 4, pl.ds(at, 8), :] = (scale * f0[p, pl.ds(y, 8), :]) * new

    for bufs, cps in (((f0, f1), f_cps), ((a0, a1), a_cps)):
        for cp in cps:
            cp.wait()
        for k in range(SWEEPS):
            src, dst = bufs[k % 2], bufs[1 - k % 2]
            if k < SWEEPS - 1:
                sweep(src, k, 8, tiles, into(dst))
            elif src is f1:
                sweep(src, k, 16, rows // 8, into(dst))
            else:
                sweep(src, k, 16, rows // 8, product)


def deep_call(meta, fwd, adj, absn, near, far, chunk):
    sends, offset, rows = chunk
    ny = fwd.shape[1]
    any_spec = pl.BlockSpec(memory_space=pl.ANY)
    return pl.pallas_call(
        functools.partial(deep_kernel, sends=sends, offset=offset, rows=rows, ny=ny),
        out_shape=jax.ShapeDtypeStruct((8, rows, 128), F32),
        in_specs=[pl.BlockSpec(memory_space=pltpu.SMEM)] + [any_spec] * 5,
        out_specs=pl.BlockSpec(memory_space=pltpu.VMEM),
        scratch_shapes=[
            pltpu.VMEM((16, rows + 32, 128), F32),
            pltpu.VMEM((16, rows + 32, 128), F32),
            pltpu.VMEM((16, rows + 32, 128), F32),
            pltpu.VMEM((16, rows + 32, 128), F32),
            pltpu.VMEM((16, rows + 32, 128), F32),
            pltpu.SemaphoreType.DMA((3, 3)),
        ],
    )(meta, fwd, adj, absn, near, far)


def final_kernel(*refs, n_own, n_got):
    own = refs[:n_own]
    got = refs[n_own : n_own + n_got]
    keep, recv, out, packed = refs[n_own + n_got :]
    x = pl.program_id(0)

    @pl.when(x == 0)
    def _():
        both = keep[...] + recv[...]
        for v in range(both.shape[1] // 128):
            cols = both[:, 128 * v : 128 * v + 128]
            cols = jnp.concatenate([cols, cols], axis=0)
            packed[128 * v : 128 * v + 128, :] = cols.T

    def cover(parts):
        at = 0
        found = []
        for ref in parts:
            found.append((at, ref.shape[1], ref))
            at += ref.shape[1]
        return found

    cuts = sorted({a for a, _, _ in cover(own)} | {a for a, _, _ in cover(got)} | {out.shape[1]})

    def piece(parts, a, b):
        for at, size, ref in cover(parts):
            if at <= a and b <= at + size:
                return ref[0, a - at : b - at, :]

    for a, b in zip(cuts[:-1], cuts[1:]):
        shallow = pltpu.roll(packed[a:b, :], (128 - 8 * x) % 128, axis=1)
        deep = piece(own, a, b) + piece(got, a, b)
        out[0, a:b, :] = jnp.where(iota((b - a, 128), 1) < 4, shallow, deep)


def final_call(own, got, keep, recv):
    half = keep.shape[1]

    def spec(a):
        return pl.BlockSpec((1, a.shape[1], 128), lambda x: (x, 0, 0))

    whole = pl.BlockSpec((64, half), lambda x: (0, 0))
    return pl.pallas_call(
        functools.partial(final_kernel, n_own=len(own), n_got=len(got)),
        out_shape=jax.ShapeDtypeStruct((8, half, 128), F32),
        grid=(8,),
        in_specs=[spec(a) for a in own + got] + [whole, whole],
        out_specs=pl.BlockSpec((1, half, 128), lambda x: (x, 0, 0)),
        scratch_shapes=[pltpu.VMEM((half, 128), F32)],
        name="final",
    )(*own, *got, keep, recv)


def after(value, *others):
    return lax.optimization_barrier((value, others))[0]


def shards(pattern_index, patterns, freq_bins, absorption, forward_start, adjoint_start, measured):
    ny = forward_start.shape[2]
    parts = lax.axis_size(GX)
    total_x = parts * 8
    fwd = forward_start[0]
    adj = adjoint_start[0]
    gx = lax.axis_index(GX)
    meta = jnp.stack(
        [
            lax.axis_index("pat"),
            (gx > 0).astype(jnp.int32),
            (gx < parts - 1).astype(jnp.int32),
            pattern_index[0],
            gx % 2,
        ]
    ).astype(jnp.int32)

    lid = [[p * parts + g for g in range(parts)] for p in range(2)]
    near_pairs = [(r[g], r[g ^ 1]) for r in lid for g in range(parts)]
    far_pairs = []
    for r in lid:
        for g in range(1, parts - 1, 2):
            far_pairs += [(r[g], r[g + 1]), (r[g + 1], r[g])]
    pat_pairs = [(lid[p][g], lid[1 - p][g]) for p in range(2) for g in range(parts)]

    def exchange(near, far):
        near = lax.ppermute(near, ALL, near_pairs)
        far = lax.ppermute(far, ALL, far_pairs)
        return near, far

    out = faces_call(meta, fwd, adj, absorption, CHUNKS[0])
    halos = [exchange(*out)]
    meta = after(meta, *out)
    out = pack_call(meta, fwd, adj, absorption, patterns, CHUNKS[1:])
    t1, t2, src, near, far = out[-5:]
    meta = after(meta, near, far)
    near, far = exchange(near, far)
    for c in range(1, len(CHUNKS)):
        halos.append(exchange(*out[2 * c - 2 : 2 * c]))

    def table(phase):
        angle = 2.0 * math.pi / total_x * (phase % total_x).astype(F32)
        scale = math.sqrt(total_x)
        return jnp.cos(angle) / scale, -(jnp.sin(angle) / scale)

    bins = after(freq_bins, meta)
    x_at = jnp.arange(parts, dtype=jnp.int32) * 8
    x_in = jnp.arange(8, dtype=jnp.int32)[:, None] + x_at[None, :]
    x_out = (jnp.arange(-4, 12, dtype=jnp.int32)[:, None] + x_at[None, :]).reshape(-1)
    to_data = jnp.concatenate(table(bins[None, :, None] * x_in[:, None, :]), axis=1)
    to_data = to_data.reshape(8 * 32, parts)
    from_data = jnp.concatenate(table(bins[:, None] * x_out[None, :]), axis=0)
    seen = jnp.tile(after(measured, meta).reshape(32, 16), (1, 8))
    meta = after(meta, to_data, from_data, seen)

    own, arrived = [], []

    def deep(meta, c):
        terms = deep_call(meta, fwd, adj, absorption, *halos[c], CHUNKS[c])
        if CHUNKS[c][0]:
            arrived.append(lax.ppermute(terms, ALL, pat_pairs))
        else:
            own.append(terms)
        return after(meta, terms)

    meta = deep(meta, 0)
    fsh, surf = vmem_call(
        functools.partial(forward_kernel, ny=ny), [(8, 8, ny), (parts, 128)], shallow_scratch(ny), 5
    )(meta, t1, t2, src, near, far)
    meta = after(meta, surf)
    got = lax.all_to_all(surf, GX, 0, 0, tiled=True)
    meta = deep(meta, 1)
    model, rows = vmem_call(data_kernel, [(32, 128), (parts, 256)], [], 4)(
        meta, got, to_data, from_data, seen
    )
    meta = after(meta, rows)
    back = lax.all_to_all(rows, GX, 0, 0, tiled=True)
    for c in range(2, len(CHUNKS)):
        meta = deep(meta, c)
    send, keep = vmem_call(
        functools.partial(adjoint_kernel, ny=ny),
        [(64, ny // 2), (64, ny // 2)],
        shallow_scratch(ny) + [pltpu.VMEM((64, ny), F32)],
        6,
    )(meta, t1, t2, back, near, far, fsh)
    recv = lax.ppermute(send, ALL, pat_pairs)
    gradient = final_call(own, arrived, keep, recv)
    return (gradient, model[:, :16].reshape(1, 2, 16, 16))


def solution(mesh):
    torus = Mesh(mesh.devices.reshape(mesh.shape["pat"], 4, 2, 4, 2), ALL)
    in_specs = (
        P("pat"),
        P(None, GX, None),
        P(),
        P(GX, None, None),
        P("pat", GX, None, None),
        P("pat", GX, None, None),
        P("pat", None, None, GX),
    )
    out_specs = (P(GX, "pat", None), P("pat", None, None, GX))

    return jax.shard_map(
        shards, mesh=torus, in_specs=in_specs, out_specs=out_specs, check_vma=False
    )
```

time: 289 us -> 211 us (0.73)
  Pallas kernels: 0 us -> 83.2 us
  other arithmetic: 62.1 us -> 2.09 us
  waiting for transfers between devices: 129 us -> 73.1 us
  blocking collectives: 26.6 us -> 0 us
  starting transfers between devices: 54 us -> 42.7 us
  local copies, waits for them, and re-layouts: 12.4 us -> 6.41 us
    pallas_call x0 -> x9, Pallas kernels: none -> 83.2 us  [the longest x3 47.2 us: deep_call(): pl.pallas_call(functools.partial(deep_kernel, sends=sends, offset=offset,...]
    add x7 -> x3, other arithmetic: 50.4 us -> 0.08 us  [the longest x2 0.08 us: shards(): jnp.arange(-4, 12, dtype=jnp.int32)[:, None] + x_at[None, :]]
    ppermute x16 -> x11, waiting for transfers between devices: 88.1 us -> 45.3 us  [the longest x4 38.2 us: exchange(): far = lax.ppermute(far, ALL, far_pairs)]
    all_to_all x3 -> x0, blocking collectives: 26.6 us -> none  [moved_by_axis(): filled = lax.all_to_all(filled, axes[k], k, k, tiled=True)]
    ppermute x16 -> x11, starting transfers between devices: 42.5 us -> 26.8 us  [the longest x4 23.2 us: exchange(): far = lax.ppermute(far, ALL, far_pairs)]
    all_to_all x2, waiting for transfers between devices: 40.7 us -> 27.8 us  [the longest x1 19.3 us: shards(): got = lax.all_to_all(surf, GX, 0, 0, tiled=True)]
    neg x1 -> x0, other arithmetic: 4.78 us -> none  [shards(): local_terms = -jnp.sum(fluence * adjoint, axis=0)]
    all_to_all x2, starting transfers between devices: 11.5 us -> 15.9 us  [the longest x1 9.52 us: shards(): got = lax.all_to_all(surf, GX, 0, 0, tiled=True)]
  transfers between devices with their start and end apart: 18 -> 13, of which waited for: 15 -> 5; matrix products, arithmetic and copies ran while one was open for 3% -> 2% of each run, Pallas kernels for 0% -> 35%
where the time goes in v1:
time: 211 us; the launch traced here: 209 us
  Pallas kernels  83.2 us (39%)
  waiting for transfers between devices  73.1 us (35%)
  starting transfers between devices  42.7 us (20%)
  local copies, waits for them, and re-layouts  6.41 us (3%)
    pallas_call x3, Pallas kernels, deep_call(): pl.pallas_call(functools.partial(deep_kernel, sends=sends, offset=offset,...  47.2 us
    ppermute x4, waiting for transfers between devices, exchange(): far = lax.ppermute(far, ALL, far_pairs)  38.2 us
    ppermute x4, starting transfers between devices, exchange(): far = lax.ppermute(far, ALL, far_pairs)  23.2 us
    all_to_all x1, waiting for transfers between devices, shards(): got = lax.all_to_all(surf, GX, 0, 0, tiled=True)  19.3 us
    pallas_call x1, Pallas kernels, pack_call(): pl.pallas_call(functools.partial(pack_kernel, chunks=chunks, ny=ny), out_...  12.3 us
    all_to_all x1, starting transfers between devices, shards(): got = lax.all_to_all(surf, GX, 0, 0, tiled=True)  9.52 us
    all_to_all x1, waiting for transfers between devices, shards(): back = lax.all_to_all(rows, GX, 0, 0, tiled=True)  8.57 us
    pallas_call x1, Pallas kernels, final_call(): pl.pallas_call(functools.partial(final_kernel, n_own=len(own), n_got=len(...  6.77 us
  transfers between devices with their start and end apart: 13, of which 5 were waited for; matrix products, arithmetic and copies ran while one was open for 2% of the time, Pallas kernels for 35%

profile of v1, /device:TPU:32, one launch (start us, length us, event | category | flops | bytes accessed | tf_op | source)
XLA Modules:
  0.0 209.0 jit_solution(10550471898271256918)
XLA Ops:
  1.3 0.6 stack.27.meta
  1.9 4.3 %faces.1 = (f32[11,272,128]{2,1,0:T(8,128)}, f32[11,272,128]{2,1,0:T(8,128)}) custom-call(s32[5]{0:T(128)} %stack.27.meta, f32[8,1024,128]{2,1,0:T(8,128)} %bitcast.19, f32[8,1024,128]{2,1,0:T(8,128)} %bitcast.24, f32[8,1024,128]{2,1,0:T(8,128)} %absn.9), custom_call_target="tpu_custom_call" | custom-call | tf_op jit(solution)/shard_map/faces/pallas_call | solution.py:76
  6.2 0.1 collective-permute-start
  6.3 0.0 copy-start.5
  6.3 0.0 copy-start.4
  6.3 12.3 %pack.1 = (f32[11,272,128]{2,1,0:T(8,128)}, f32[11,272,128]{2,1,0:T(8,128)}, f32[11,520,128]{2,1,0:T(8,128)}, f32[11,520,128]{2,1,0:T(8,128)}, f32[128,1024]{1,0...) custom-call(s32[5]{0:T(128)} %stack.27.meta, ...), custom_call_target="tpu_custom_call" | custom-call | tf_op jit(solution)/shard_map/pack/pallas_call | solution.py:168
  18.6 0.5 collective-permute-start.6
  19.2 6.6 %collective-permute-start.7 = (f32[11,520,128]{2,1,0:T(8,128)}, f32[11,520,128]{2,1,0:T(8,128)}, u32[]{:S(2)}, u32[]{:S(2)}) collective-permute-start(f32[11,520,128]{2,1,0:T(8,128)} %get-tuple-element.50), channel_id=1, source_target_pairs={{1,2},{2,1},{3,4},{4,3},{5,6},{6,5},{7,8},{8,7},{9,10},{10,9},{11,... | collective-permute-start | bytes 8785928 | tf_op jit(solution)/shard_map/ppermute | solution.py:548
  25.8 3.5 %collective-permute-start.1 = (f32[11,272,128]{2,1,0:T(8,128)}, f32[11,272,128]{2,1,0:T(8,128)}, u32[]{:S(2)}, u32[]{:S(2)}) collective-permute-start(f32[11,272,128]{2,1,0:T(8,128)} %get-tuple-element.30), channel_id=1, source_target_pairs={{1,2},{2,1},{3,4},{4,3},{5,6},{6,5},{7,8},{8,7},{9,10},{10,9},{11,... | collective-permute-start | bytes 4595720 | tf_op jit(solution)/shard_map/ppermute | solution.py:548
  29.3 0.1 collective-permute-start.2
  29.4 1.9 collective-permute-done.2.near
  31.3 0.1 collective-permute-start.4
  31.4 0.0 collective-permute-done.near
  31.4 6.6 %collective-permute-start.5 = (f32[11,272,128]{2,1,0:T(8,128)}, f32[11,272,128]{2,1,0:T(8,128)}, u32[]{:S(2)}, u32[]{:S(2)}) collective-permute-start(f32[11,272,128]{2,1,0:T(8,128)} %get-tuple-element.45), channel_id=1, source_target_pairs={{1,2},{2,1},{3,4},{4,3},{5,6},{6,5},{7,8},{8,7},{9,10},{10,9},{11,... | collective-permute-start | bytes 4595720 | tf_op jit(solution)/shard_map/ppermute | solution.py:548
  38.0 0.1 broadcast_add_fusion
  38.1 0.1 add.81
  38.2 0.3 cosine_multiply_fusion
  38.5 38.2 %collective-permute-done.1.far = f32[11,272,128]{2,1,0:T(8,128)} collective-permute-done((f32[11,272,128]{2,1,0:T(8,128)}, f32[11,272,128]{2,1,0:T(8,128)}, u32[]{:S(2)}, u32[]{:S(2)}) %collective-permute-start.1) | collective-permute-done | bytes 1531936 | tf_op jit(solution)/shard_map/ppermute | solution.py:548
  76.7 6.6 %collective-permute-start.3 = (f32[96,1024]{1,0:T(8,128)}, f32[96,1024]{1,0:T(8,128)}, u32[]{:S(2)}, u32[]{:S(2)}) collective-permute-start(f32[96,1024]{1,0:T(8,128)} %get-tuple-element.33), channel_id=1, source_target_pairs={{1,2},{2,1},{3,4},{4,3},{5,6},{6,5},{7,8},{8,7},{9,10},{10,9},{11,... | collective-permute-start | bytes 1179656 | tf_op jit(solution)/shard_map/ppermute | solution.py:548
  83.3 0.7 pad_maximum_fusion.1.back
  83.9 0.1 copy.11
  84.0 0.3 cosine_multiply_fusion.1
  84.3 0.7 pad_maximum_fusion
  85.0 13.3 %shard_map.86 = f32[8,256,128]{2,1,0:T(8,128)} custom-call(s32[5]{0:T(128)} %stack.27.meta, f32[8,1024,128]{2,1,0:T(8,128)} %bitcast.21, f32[8,1024,128]{2,1,0:T(8,128)} %bitcast.26, f32[8,1024,128]{2,1,0:T(8,128)} %absn.9, f32[11,272,128]{2,1,0:T(8,128)} %collective-permute-done.near, f32[11,272,128]{2,1,0:T(8,128)} %collective-permute-done.1.far), custom_call_target="tpu_custom_call" | custom-call | tf_op jit(solution)/shard_map/pallas_call | solution.py:448
  98.3 0.0 collective-permute-done.3.far
  98.3 0.7 collective-permute-start.8
  99.0 4.9 %shard_map.87 = (f32[8,8,1024]{2,1,0:T(8,128)}, f32[64,128]{1,0:T(8,128)}) custom-call(s32[5]{0:T(128)} %stack.27.meta, f32[128,1024]{1,0:T(8,128)} %get-tuple-element.39.t1, f32[64,1024]{1,0:T(8,128)} %get-tuple-element.40.t2, f32[8,1024]{1,0:T(8,128)} %get-tuple-element.41.src, f32[96,1024]{1,0:T(8,128)} %copy-done.1, f32[96,1024]{1,0:T(8,128)} %collective-permute-done.3.far), custom_call_target="tpu_custom_call" | custom-call | tf_op jit(solution)/shard_map/pallas_call | solution.py:587
  103.9 0.0 collective-permute-done.4.near
  103.9 0.0 collective-permute-done.5.far
  103.9 13.2 %shard_map.88 = f32[8,256,128]{2,1,0:T(8,128)} custom-call(s32[5]{0:T(128)} %stack.27.meta, f32[8,1024,128]{2,1,0:T(8,128)} %bitcast.22, f32[8,1024,128]{2,1,0:T(8,128)} %bitcast.27, f32[8,1024,128]{2,1,0:T(8,128)} %absn.9, f32[11,272,128]{2,1,0:T(8,128)} %collective-permute-done.4.near, f32[11,272,128]{2,1,0:T(8,128)} %collective-permute-done.5.far), custom_call_target="tpu_custom_call" | custom-call | tf_op jit(solution)/shard_map/pallas_call | solution.py:448
  117.1 1.5 collective-permute-start.9
  118.6 9.5 %all-to-all-start = ((f32[64,1,128]{2,1,0:T(1,128)}), f32[64,1,128]{2,1,0:T(1,128)S(1)}, u32[]{:S(2)}, u32[]{:S(2)}) async-start(f32[64,1,128]{2,1,0:T(1,128)} %bitcast.10), calls=%async_computation | async-start | bytes 65536 | tf_op jit(solution)/shard_map/all_to_all | solution.py:591
  128.2 0.7 copy.13.measured
  128.8 19.3 %all-to-all-done = f32[64,1,128]{2,1,0:T(1,128)S(1)} async-done(((f32[64,1,128]{2,1,0:T(1,128)}), f32[64,1,128]{2,1,0:T(1,128)S(1)}, u32[]{:S(2)}, u32[]{:S(2)}) %all-to-all-start) | async-done | bytes 32800 | tf_op jit(solution)/shard_map/all_to_all | solution.py:591
  148.1 0.6 copy-done.3
  148.7 2.8 %shard_map.89 = (f32[32,128]{1,0:T(8,128)}, f32[64,256]{1,0:T(8,128)}) custom-call(s32[5]{0:T(128)} %stack.27.meta, f32[64,128]{1,0:T(8,128)} %bitcast.32, f32[256,64]{1,0:T(8,128)} %bitcast.29, f32[32,1024]{1,0:T(8,128)} %pad_maximum_fusion.1.back, f32[32,128]{1,0:T(8,128)} %copy.13.measured), custom_call_target="tpu_custom_call" | custom-call | tf_op jit(solution)/shard_map/pallas_call | solution.py:593
  151.5 1.5 copy.14
  153.0 6.4 %all-to-all-start.1 = ((f32[64,1,256]{2,1,0:T(1,128)}), f32[64,1,256]{2,1,0:T(1,128)S(1)}, u32[]{:S(2)}, u32[]{:S(2)}) async-start(f32[64,1,256]{2,1,0:T(1,128)} %copy.14), calls=%async_computation.1 | async-start | bytes 131072 | tf_op jit(solution)/shard_map/all_to_all | solution.py:597
  159.4 8.6 %all-to-all-done.1 = f32[64,1,256]{2,1,0:T(1,128)S(1)} async-done(((f32[64,1,256]{2,1,0:T(1,128)}), f32[64,1,256]{2,1,0:T(1,128)S(1)}, u32[]{:S(2)}, u32[]{:S(2)}) %all-to-all-start.1) | async-done | bytes 65568 | tf_op jit(solution)/shard_map/all_to_all | solution.py:597
  168.0 0.6 copy.17
  168.6 0.0 collective-permute-done.6.near
  168.6 1.6 copy-done
  170.3 20.7 %shard_map.90.refs_0_ = f32[8,512,128]{2,1,0:T(8,128)} custom-call(s32[5]{0:T(128)} %stack.27.meta, f32[8,1024,128]{2,1,0:T(8,128)} %bitcast.23, f32[8,1024,128]{2,1,0:T(8,128)} %bitcast.28, f32[8,1024,128]{2,1,0:T(8,128)} %absn.9, f32[11,520,128]{2,1,0:T(8,128)} %copy-done, f32[11,520,128]{2,1,0:T(8,128)} %collective-permute-done.7.far), custom_call_target="tpu_custom_call" | custom-call | tf_op jit(solution)/shard_map/pallas_call | solution.py:448
  190.9 5.0 %shard_map.91 = (f32[64,512]{1,0:T(8,128)}, f32[64,512]{1,0:T(8,128)}) custom-call(s32[5]{0:T(128)} %stack.27.meta, f32[128,1024]{1,0:T(8,128)} %get-tuple-element.39.t1, f32[64,1024]{1,0:T(8,128)} %get-tuple-element.40.t2, f32[64,256]{1,0:T(8,128)} %bitcast.31, f32[96,1024]{1,0:T(8,128)} %copy-done.1, f32[96,1024]{1,0:T(8,128)} %collective-permute-done.3.far, ...), custom_call_target="tpu_custom_call" | custom-call | tf_op jit(solution)/shard_map/pallas_call | solution.py:600
  195.9 0.5 collective-permute-start.10
  196.4 5.2 %collective-permute-done.10.refs_4_ = f32[64,512]{1,0:T(8,128)S(1)} collective-permute-done((f32[64,512]{1,0:T(8,128)}, f32[64,512]{1,0:T(8,128)S(1)}, u32[]{:S(2)}, u32[]{:S(2)}) %collective-permute-start.10) | collective-permute-done | bytes 131104 | tf_op jit(solution)/shard_map/ppermute | solution.py:606
  201.6 0.7 copy-done.2
  202.3 6.8 %final.1 = f32[8,512,128]{2,1,0:T(8,128)} custom-call(f32[8,512,128]{2,1,0:T(8,128)} %shard_map.90.refs_0_, f32[8,256,128]{2,1,0:T(8,128)} %collective-permute-done.8.refs_1_, f32[8,256,128]{2,1,0:T(8,128)} %collective-permute-done.9.refs_2_, f32[64,512]{1,0:T(8,128)} %get-tuple-element.53.refs_3_, f32[64,512]{1,0:T(8,128)} %copy-done.2), custom_call_target="tpu_custom_call" | custom-call | tf_op jit(solution)/shard_map/final/pallas_call | solution.py:506
  (14 shorter events, 0.0 us)
Async XLA Ops:
  6.2 25.2 %collective-permute-start = (f32[11,272,128]{2,1,0:T(8,128)}, f32[11,272,128]{2,1,0:T(8,128)}, u32[]{:S(2)}, u32[]{:S(2)}) collective-permute-start(f32[11,272,128]{2,1,0:T(8,128)} %get-tuple-element.29), channel_id=1, source_target_pairs={{0,1},{1,0},{2,3},{3,2},{4,5},{5,4},{6,7},{7,6},{8,9},{9,8},{10,11... | collective-permute-start | bytes 4595720 | tf_op jit(solution)/shard_map/ppermute | solution.py:547
  6.3 31.9 %copy-start.5 = (s32[16]{0:T(128)S(1)}, s32[16]{0:T(128)}, u32[]{:S(2)}) copy-start(s32[16]{0:T(128)} %param.9) | copy-start | bytes 196
  6.3 77.6 %copy-start.4 = (f32[1,2,16,16]{3,2,1,0:T(8,128)S(1)}, f32[1,2,16,16]{3,2,1,0:T(8,128)}, u32[]{:S(2)}) copy-start(f32[1,2,16,16]{3,2,1,0:T(8,128)} %param.13) | copy-start | bytes 6148
  18.6 150.0 %collective-permute-start.6 = (f32[11,520,128]{2,1,0:T(8,128)}, f32[11,520,128]{2,1,0:T(8,128)S(1)}, u32[]{:S(2)}, u32[]{:S(2)}) collective-permute-start(f32[11,520,128]{2,1,0:T(8,128)} %get-tuple-element.49), channel_id=1, source_target_pairs={{0,1},{1,0},{2,3},{3,2},{4,5},{5,4},{6,7},{7,6},{8,9},{9,8},{10,11... | collective-permute-start | bytes 8785928 | tf_op jit(solution)/shard_map/ppermute | solution.py:547
  19.2 149.5 %collective-permute-start.7 = (f32[11,520,128]{2,1,0:T(8,128)}, f32[11,520,128]{2,1,0:T(8,128)}, u32[]{:S(2)}, u32[]{:S(2)}) collective-permute-start(f32[11,520,128]{2,1,0:T(8,128)} %get-tuple-element.50), channel_id=1, source_target_pairs={{1,2},{2,1},{3,4},{4,3},{5,6},{6,5},{7,8},{8,7},{9,10},{10,9},{11,... | collective-permute-start | bytes 8785928 | tf_op jit(solution)/shard_map/ppermute | solution.py:548
  25.8 50.9 %collective-permute-start.1 = (f32[11,272,128]{2,1,0:T(8,128)}, f32[11,272,128]{2,1,0:T(8,128)}, u32[]{:S(2)}, u32[]{:S(2)}) collective-permute-start(f32[11,272,128]{2,1,0:T(8,128)} %get-tuple-element.30), channel_id=1, source_target_pairs={{1,2},{2,1},{3,4},{4,3},{5,6},{6,5},{7,8},{8,7},{9,10},{10,9},{11,... | collective-permute-start | bytes 4595720 | tf_op jit(solution)/shard_map/ppermute | solution.py:548
  29.3 2.0 collective-permute-start.2
  31.3 67.0 %copy-start.1 = (f32[96,1024]{1,0:T(8,128)}, f32[96,1024]{1,0:T(8,128)S(1)}, u32[]{:S(2)}) copy-start(f32[96,1024]{1,0:T(8,128)S(1)} %collective-permute-done.2.near) | copy-start | bytes 1179652
  31.3 72.6 %collective-permute-start.4 = (f32[11,272,128]{2,1,0:T(8,128)}, f32[11,272,128]{2,1,0:T(8,128)}, u32[]{:S(2)}, u32[]{:S(2)}) collective-permute-start(f32[11,272,128]{2,1,0:T(8,128)} %get-tuple-element.44), channel_id=1, source_target_pairs={{0,1},{1,0},{2,3},{3,2},{4,5},{5,4},{6,7},{7,6},{8,9},{9,8},{10,11... | collective-permute-start | bytes 4595720 | tf_op jit(solution)/shard_map/ppermute | solution.py:547
  31.4 72.5 %collective-permute-start.5 = (f32[11,272,128]{2,1,0:T(8,128)}, f32[11,272,128]{2,1,0:T(8,128)}, u32[]{:S(2)}, u32[]{:S(2)}) collective-permute-start(f32[11,272,128]{2,1,0:T(8,128)} %get-tuple-element.45), channel_id=1, source_target_pairs={{1,2},{2,1},{3,4},{4,3},{5,6},{6,5},{7,8},{8,7},{9,10},{10,9},{11,... | collective-permute-start | bytes 4595720 | tf_op jit(solution)/shard_map/ppermute | solution.py:548
  76.7 21.6 %collective-permute-start.3 = (f32[96,1024]{1,0:T(8,128)}, f32[96,1024]{1,0:T(8,128)}, u32[]{:S(2)}, u32[]{:S(2)}) collective-permute-start(f32[96,1024]{1,0:T(8,128)} %get-tuple-element.33), channel_id=1, source_target_pairs={{1,2},{2,1},{3,4},{4,3},{5,6},{6,5},{7,8},{8,7},{9,10},{10,9},{11,... | collective-permute-start | bytes 1179656 | tf_op jit(solution)/shard_map/ppermute | solution.py:548
  98.3 98.1 %collective-permute-start.8 = (f32[8,256,128]{2,1,0:T(8,128)}, f32[8,256,128]{2,1,0:T(8,128)}, u32[]{:S(2)}, u32[]{:S(2)}) collective-permute-start(f32[8,256,128]{2,1,0:T(8,128)} %shard_map.86), channel_id=1, source_target_pairs={{0,64},{1,65},{2,66},{3,67},{4,68},{5,69},{6,70},{7,71},{8,72},{9,... | collective-permute-start | bytes 3145736 | tf_op jit(solution)/shard_map/ppermute | solution.py:581
  117.1 79.3 %collective-permute-start.9 = (f32[8,256,128]{2,1,0:T(8,128)}, f32[8,256,128]{2,1,0:T(8,128)}, u32[]{:S(2)}, u32[]{:S(2)}) collective-permute-start(f32[8,256,128]{2,1,0:T(8,128)} %shard_map.88), channel_id=1, source_target_pairs={{0,64},{1,65},{2,66},{3,67},{4,68},{5,69},{6,70},{7,71},{8,72},{9,... | collective-permute-start | bytes 3145736 | tf_op jit(solution)/shard_map/ppermute | solution.py:581
  118.6 29.5 %all-to-all-start = ((f32[64,1,128]{2,1,0:T(1,128)}), f32[64,1,128]{2,1,0:T(1,128)S(1)}, u32[]{:S(2)}, u32[]{:S(2)}) async-start(f32[64,1,128]{2,1,0:T(1,128)} %bitcast.10), calls=%async_computation | async-start | bytes 65536 | tf_op jit(solution)/shard_map/all_to_all | solution.py:591
  148.1 0.6 copy-start.3
  153.0 15.0 %all-to-all-start.1 = ((f32[64,1,256]{2,1,0:T(1,128)}), f32[64,1,256]{2,1,0:T(1,128)S(1)}, u32[]{:S(2)}, u32[]{:S(2)}) async-start(f32[64,1,256]{2,1,0:T(1,128)} %copy.14), calls=%async_computation.1 | async-start | bytes 131072 | tf_op jit(solution)/shard_map/all_to_all | solution.py:597
  168.6 1.6 copy-start
  195.9 5.7 %collective-permute-start.10 = (f32[64,512]{1,0:T(8,128)}, f32[64,512]{1,0:T(8,128)S(1)}, u32[]{:S(2)}, u32[]{:S(2)}) collective-permute-start(f32[64,512]{1,0:T(8,128)} %get-tuple-element.54), channel_id=1, source_target_pairs={{0,64},{1,65},{2,66},{3,67},{4,68},{5,69},{6,70},{7,71},{8,72},{9,... | collective-permute-start | bytes 393224 | tf_op jit(solution)/shard_map/ppermute | solution.py:606
  201.6 0.7 copy-start.2

commit v2 on v1

--- a/solution.py
+++ b/solution.py
@@ -15,6 +15,9 @@
 CHUNKS = ((True, 0, 256), (True, 256, 256), (False, 0, 512))
 HIGH = lax.Precision.HIGHEST
 F32 = jnp.float32
+BF16 = jnp.bfloat16
+MXU_PLANES = (1,)
+PLANES = 2
 
 
 def sweep_weight(sweep):
@@ -53,41 +56,18 @@
     return outs
 
 
-def faces_kernel(meta, fwd, adj, absn, near, far, fs, ad, ab, in_sem, sem, *, chunk, ny):
-    sends, offset, rows = chunk
-    nh = halo_rows(rows, ny)
-    y0 = chunk_start(meta, sends, offset, ny // 2)
-    s = pl.multiple_of(jnp.clip(y0 - 8, 0, ny - nh), 8)
-    loads = []
-    for i, (h, v) in enumerate(((fwd, fs), (adj, ad), (absn, ab))):
-        cp = pltpu.make_async_copy(h.at[:, pl.ds(s, nh), :], v, in_sem.at[i])
-        cp.start()
-        loads.append(cp)
-    for cp in loads:
-        cp.wait()
-    for cp in face_copies(meta, (fs, ad, ab), s, near, far, sem, chunk, ny):
-        cp.wait()
-
-
-def faces_call(meta, fwd, adj, absn, chunk):
-    ny = fwd.shape[1]
-    nh = halo_rows(chunk[2], ny)
-    any_spec = pl.BlockSpec(memory_space=pl.ANY)
-    return pl.pallas_call(
-        functools.partial(faces_kernel, chunk=chunk, ny=ny),
-        out_shape=[jax.ShapeDtypeStruct((11, nh, 128), F32)] * 2,
-        in_specs=[pl.BlockSpec(memory_space=pltpu.SMEM)] + [any_spec] * 3,
-        out_specs=[any_spec] * 2,
-        scratch_shapes=[pltpu.VMEM((8, nh, 128), F32)] * 3
-        + [pltpu.SemaphoreType.DMA((3,)), pltpu.SemaphoreType.DMA((2, 3))],
-        name="faces",
-    )(meta, fwd, adj, absn)
-
-
-def pack_kernel(meta, fwd, adj, absn, pats, *rest, chunks, ny):
+SHALLOW_ROWS = 96
+
+
+def shallow_place(v, row, nh):
+    at = SHALLOW_ROWS * v + row
+    return at // nh, at % nh
+
+
+def head_kernel(meta, fwd, adj, absn, pats, *rest, chunks, ny):
     n = 2 * len(chunks)
     faces = rest[:n]
-    t1, t2, src, near, far, fs, ad, ab, p1, p2, in_sem, src_sem, face_sem = rest[n:]
+    t1, t2, src, fs, ad, ab, near, far, in_sem, src_sem, face_sem, sh_sem = rest[n:]
     loads = []
     for i, (h, v) in enumerate(((fwd, fs), (adj, ad), (absn, ab))):
         cp = pltpu.make_async_copy(h, v, in_sem.at[i])
@@ -95,53 +75,50 @@
         loads.append(cp)
     src_cp = pltpu.make_async_copy(pats.at[meta[3]], src, src_sem)
     src_cp.start()
-    lane = iota((8, 128), 1)
-    un = 8
-
-    def pack(parts, dst):
-        def body(t, carry):
-            done = []
-            for u in range(un):
-                y = pl.multiple_of((t * un + u) * 8, 8)
-                acc = jnp.zeros((8, 128), F32)
-                for arr, base in parts:
-                    for x in range(8):
-                        at = base + 8 * x
-                        v = arr[x, pl.ds(y, 8), :]
-                        v = pltpu.roll(v, at, axis=1) if at else v
-                        acc = jnp.where((lane >= at) & (lane < at + 8), v, acc)
-                done.append((y, acc))
-            for y, acc in done:
-                dst[pl.ds(y, 8), :] = acc
+
+    def pack(arr, dst, base):
+        def body(x, carry):
+            at = pl.multiple_of(base + 8 * x, 8)
+            for v in range(ny // 128):
+                dst[pl.ds(at, 8), 128 * v : 128 * v + 128] = arr[x, 128 * v : 128 * v + 128, :].T[:8]
             return carry
 
-        lax.fori_loop(0, ny // (8 * un), body, 0)
-
-    for cp in loads:
-        cp.wait()
+        lax.fori_loop(0, 8, body, 0)
+
+    loads[0].wait()
+    pack(fs, t1, 0)
+    loads[1].wait()
+    pack(ad, t1, 64)
+    loads[2].wait()
     outs = []
     for c, chunk in enumerate(chunks):
         outs += face_copies(
             meta, (fs, ad, ab), 0, faces[2 * c], faces[2 * c + 1], face_sem.at[c], chunk, ny
         )
-    pack(((fs, 0), (ad, 64)), p1)
-    pack(((ab, 0),), p2)
-    for v in range(ny // 128):
-        t1[:, v * 128 : (v + 1) * 128] = p1[v * 128 : (v + 1) * 128, :].T
-        t2[:, v * 128 : (v + 1) * 128] = p2[v * 128 : (v + 1) * 128, :].T[:64]
+    pack(ab, t2, 0)
     src_cp.wait()
+    nh = halo_rows(chunks[0][2], ny)
+
+    def put(dst, value, row):
+        for v in range(ny // 128):
+            p, r = shallow_place(v, row, nh)
+            dst[p, r : r + 8, :] = value[:, 128 * v : 128 * v + 128]
 
     def high_face(dst):
-        dst[0:32, :] = t1[32:64, :]
-        dst[32:64, :] = t1[96:128, :]
-        dst[64:88, :] = t2[40:64, :]
-        dst[88:96, :] = pltpu.roll(src[...], 3, axis=0)
+        for i in range(4):
+            put(dst, t1[32 + 8 * i : 40 + 8 * i, :], 8 * i)
+            put(dst, t1[96 + 8 * i : 104 + 8 * i, :], 32 + 8 * i)
+        for i in range(3):
+            put(dst, t2[40 + 8 * i : 48 + 8 * i, :], 64 + 8 * i)
+        put(dst, pltpu.roll(src[...], 3, axis=0), 88)
 
     def low_face(dst):
-        dst[0:32, :] = t1[0:32, :]
-        dst[32:64, :] = t1[64:96, :]
-        dst[64:88, :] = t2[0:24, :]
-        dst[88:96, :] = src[...]
+        for i in range(4):
+            put(dst, t1[8 * i : 8 * i + 8, :], 8 * i)
+            put(dst, t1[64 + 8 * i : 72 + 8 * i, :], 32 + 8 * i)
+        for i in range(3):
+            put(dst, t2[8 * i : 8 * i + 8, :], 64 + 8 * i)
+        put(dst, src[...], 88)
 
     @pl.when(meta[4] == 0)
     def _():
@@ -153,31 +130,36 @@
         low_face(near)
         high_face(far)
 
+    for i, (v, h) in enumerate(((near, faces[0]), (far, faces[1]))):
+        cp = pltpu.make_async_copy(v, h.at[pl.ds(11, 3)], sh_sem.at[i])
+        cp.start()
+        outs.append(cp)
     for cp in outs:
         cp.wait()
 
 
-def pack_call(meta, fwd, adj, absn, pats, chunks):
+def head_call(meta, fwd, adj, absn, pats, chunks):
     ny = fwd.shape[1]
-    small = [(128, ny), (64, ny), (8, ny), (96, ny), (96, ny)]
+    small = [(128, ny), (64, ny), (8, ny)]
     shapes = []
-    for _, _, rows in chunks:
-        shapes += [(11, halo_rows(rows, ny), 128)] * 2
+    for c, (_, _, rows) in enumerate(chunks):
+        shapes += [(11 if c else 14, halo_rows(rows, ny), 128)] * 2
     any_spec = pl.BlockSpec(memory_space=pl.ANY)
     vmem = pl.BlockSpec(memory_space=pltpu.VMEM)
     return pl.pallas_call(
-        functools.partial(pack_kernel, chunks=chunks, ny=ny),
+        functools.partial(head_kernel, chunks=chunks, ny=ny),
         out_shape=[jax.ShapeDtypeStruct(s, F32) for s in shapes + small],
         in_specs=[pl.BlockSpec(memory_space=pltpu.SMEM)] + [any_spec] * 4,
-        out_specs=[any_spec] * len(shapes) + [vmem] * 5,
+        out_specs=[any_spec] * len(shapes) + [vmem] * 3,
         scratch_shapes=[pltpu.VMEM((8, ny, 128), F32)] * 3
-        + [pltpu.VMEM((ny, 128), F32)] * 2
+        + [pltpu.VMEM((3, shapes[0][1], 128), F32)] * 2
         + [
             pltpu.SemaphoreType.DMA((3,)),
             pltpu.SemaphoreType.DMA(()),
             pltpu.SemaphoreType.DMA((len(chunks), 2, 3)),
+            pltpu.SemaphoreType.DMA((2,)),
         ],
-        name="pack",
+        name="head",
     )(meta, fwd, adj, absn, pats)
 
 
@@ -193,15 +175,34 @@
     return v
 
 
+def shallow_side(near, far, core0, row, ny):
+    a, b = [], []
+    for v in range(ny // 128):
+        p, r = shallow_place(v, row, near.shape[1])
+        a.append(near[p, r : r + 8, :])
+        b.append(far[p, r : r + 8, :])
+    a = jnp.concatenate(a, axis=1)
+    b = jnp.concatenate(b, axis=1)
+    return jnp.where(core0, b, a), jnp.where(core0, a, b)
+
+
+def fetch_shallow(near_hbm, far_hbm, near, far, sem):
+    cps = []
+    for i, (h, v) in enumerate(((near_hbm, near), (far_hbm, far))):
+        cp = pltpu.make_async_copy(h.at[pl.ds(11, 3)], v, sem.at[i])
+        cp.start()
+        cps.append(cp)
+    for cp in cps:
+        cp.wait()
+
+
 def shallow_solve(meta, start, at, near, far, near_at, t2, f0, f1, r, s, ny):
     lo_ok = jnp.where(meta[1] > 0, 1.0, 0.0).astype(F32)
     hi_ok = jnp.where(meta[2] > 0, 1.0, 0.0).astype(F32)
     core0 = meta[4] == 0
 
     def side(row):
-        a = near[row : row + 8, :]
-        b = far[row : row + 8, :]
-        return jnp.where(core0, b, a), jnp.where(core0, a, b)
+        return shallow_side(near, far, core0, row, ny)
 
     for i in range(4):
         f0[i], f0[12 + i] = side(near_at + 8 * i)
@@ -235,14 +236,15 @@
         lax.fori_loop(0, 7 - k, pair, 0)
 
 
-def forward_kernel(meta, t1, t2, src, near, far, fsh, surf, f0, f1, r, s, *, ny):
+def forward_kernel(
+    meta, t1, t2, src, near_hbm, far_hbm, fsh, surf, near, far, sem, f0, f1, r, s, *, ny
+):
+    fetch_shallow(near_hbm, far_hbm, near, far, sem)
     z0 = iota((8, ny), 0) == 0
-    core0 = meta[4] == 0
+    lo, hi = shallow_side(near, far, meta[4] == 0, 88, ny)
     for i in range(3):
-        a = near[88 + i : 89 + i, :]
-        b = far[88 + i : 89 + i, :]
-        s[1 + i] = jnp.where(z0, jnp.where(core0, b, a), 0.0)
-        s[12 + i] = jnp.where(z0, jnp.where(core0, a, b), 0.0)
+        s[1 + i] = jnp.where(z0, lo[i : i + 1, :], 0.0)
+        s[12 + i] = jnp.where(z0, hi[i : i + 1, :], 0.0)
     for i in range(8):
         s[4 + i] = jnp.where(z0, src[i : i + 1, :], 0.0)
     shallow_solve(meta, t1, 0, near, far, 0, t2, f0, f1, r, s, ny)
@@ -253,24 +255,30 @@
         surf[8 * v : 8 * v + 8, :] = group_transpose(top[:, 128 * v : 128 * v + 128])
 
 
-def shallow_scratch(ny):
-    return [pltpu.VMEM((16, 8, ny), F32)] * 4
-
-
-def vmem_call(kernel, out_shapes, scratch, n_in):
+def shallow_scratch(ny, nh):
+    return (
+        [pltpu.VMEM((3, nh, 128), F32)] * 2
+        + [pltpu.SemaphoreType.DMA((2,))]
+        + [pltpu.VMEM((16, 8, ny), F32)] * 4
+    )
+
+
+def vmem_call(kernel, out_shapes, scratch, n_in, n_any=0):
     vmem = pl.BlockSpec(memory_space=pltpu.VMEM)
+    any_spec = pl.BlockSpec(memory_space=pl.ANY)
     return pl.pallas_call(
         kernel,
         out_shape=[jax.ShapeDtypeStruct(s, F32) for s in out_shapes],
-        in_specs=[pl.BlockSpec(memory_space=pltpu.SMEM)] + [vmem] * n_in,
+        in_specs=[pl.BlockSpec(memory_space=pltpu.SMEM)] + [vmem] * n_in + [any_spec] * n_any,
         out_specs=[vmem] * len(out_shapes),
         scratch_shapes=scratch,
     )
 
 
 def adjoint_kernel(
-    meta, t1, t2, got, near, far, fsh, send, keep, f0, f1, r, s, prod, *, ny
+    meta, t1, t2, got, fsh, near_hbm, far_hbm, send, keep, near, far, sem, f0, f1, r, s, prod, *, ny
 ):
+    fetch_shallow(near_hbm, far_hbm, near, far, sem)
     z0 = iota((8, ny), 0) == 0
     for h in range(2):
         parts = []
@@ -295,7 +303,7 @@
         send[...] = prod[:, :half]
 
 
-def data_kernel(meta, got, table, back, measured, model, send):
+def data_kernel(meta, got, table, back, measured, model, send, seen):
     lane_group = iota((32, 128), 1) // 16
     full = jnp.dot(table[...], got[...], precision=HIGH, preferred_element_type=F32)
     acc = jnp.zeros((32, 128), F32)
@@ -304,7 +312,12 @@
     for shift in (64, 32, 16):
         acc = acc + pltpu.roll(acc, shift, axis=1)
     model[...] = acc
-    misfit = acc - measured[...]
+    seen[...] = jnp.zeros((32, 128), F32)
+    seen[:, :16] = measured[...]
+    data = seen[...]
+    for shift in (16, 32, 64):
+        data = data + pltpu.roll(data, shift, axis=1)
+    misfit = acc - data
     rows = lax.dot_general(
         back[...], misfit, (((0,), (0,)), ((), ())), precision=HIGH, preferred_element_type=F32
     )
@@ -323,7 +336,7 @@
 
 
 def deep_kernel(
-    meta, fwd, adj, absn, near, far, out, f0, f1, a0, a1, rb, sem, *, sends, offset, rows, ny
+    meta, fwd, adj, absn, near, far, out, f0, f1, a0, a1, rb, zb, sem, *, sends, offset, rows, ny
 ):
     nh = halo_rows(rows, ny)
     y0 = chunk_start(meta, sends, offset, ny // 2)
@@ -389,44 +402,48 @@
     lax.fori_loop(1, 15, invert, 0)
     edges(rb)
     last = iota((8, 128), 1) == 127
+    apart = jnp.abs(iota((128, 128), 0) - iota((128, 128), 1))
+    shifts = jnp.where(apart == 1, 1.0, 0.0).astype(BF16)
+    shifts = jnp.concatenate([shifts, shifts], axis=0)
 
     def sweep(buf, k, begin, count, store):
         w = sweep_weight(k)
-        un = tile_count(count)
 
         def pair(q, carry):
             p = k + 1 + 2 * q
-
-            def block(t, cc):
-                for u in range(un):
-                    y = pl.multiple_of(begin + (t * un + u) * 8, 8)
-                    v = [buf[p - 1 + i, pl.ds(y, 8), :] for i in range(4)]
-                    for i in range(2):
-                        c = v[i + 1]
-                        ym = buf[p + i, pl.ds(y - 1, 8), :]
-                        yp = buf[p + i, pl.ds(y + 1, 8), :]
-                        zl = pltpu.roll(c, 1, axis=1)
-                        zr = jnp.where(last, 0.0, pltpu.roll(c, 127, axis=1))
-                        nb = ((v[i] + v[i + 2]) + (ym + yp)) + (zl + zr)
-                        new = ((1.0 - w) / w) * c + rb[p + i, pl.ds(y, 8), :] * nb
-                        store(p + i, y, new)
-                return cc
-
-            return lax.fori_loop(0, count // un, block, carry)
+            for i in MXU_PLANES:
+                c = buf[p + i, begin : begin + 8 * count, :]
+                head = c.astype(BF16)
+                tail = (c - head.astype(F32)).astype(BF16)
+                both = jnp.concatenate([head, tail], axis=1)
+                zb[i, : 8 * count, :] = jnp.dot(both, shifts, preferred_element_type=F32)
+            for t in range(count):
+                y = begin + 8 * t
+                v = [buf[p - 1 + i, y : y + 8, :] for i in range(4)]
+                for i in range(2):
+                    ym = buf[p + i, y - 1 : y + 7, :]
+                    yp = buf[p + i, y + 1 : y + 9, :]
+                    if i in MXU_PLANES:
+                        zs = zb[i, 8 * t : 8 * t + 8, :]
+                    else:
+                        zr = jnp.where(last, 0.0, pltpu.roll(v[i + 1], 127, axis=1))
+                        zs = pltpu.roll(v[i + 1], 1, axis=1) + zr
+                    nb = ((v[i] + v[i + 2]) + (ym + yp)) + zs
+                    store(p + i, y, ((1.0 - w) / w) * v[i + 1] + rb[p + i, y : y + 8, :] * nb)
+            return carry
 
         lax.fori_loop(0, 7 - k, pair, 0)
 
     def into(buf):
         def store(p, y, new):
-            buf[p, pl.ds(y, 8), :] = new
+            buf[p, y : y + 8, :] = new
 
         return store
 
     scale = -math.prod(sweep_weight(k) for k in range(SWEEPS)) ** 2
 
     def product(p, y, new):
-        at = pl.multiple_of(y - 16, 8)
-        out[p - 4, pl.ds(at, 8), :] = (scale * f0[p, pl.ds(y, 8), :]) * new
+        out[p - 4, y - 16 : y - 8, :] = (scale * f0[p, y : y + 8, :]) * new
 
     for bufs, cps in (((f0, f1), f_cps), ((a0, a1), a_cps)):
         for cp in cps:
@@ -456,6 +473,7 @@
             pltpu.VMEM((16, rows + 32, 128), F32),
             pltpu.VMEM((16, rows + 32, 128), F32),
             pltpu.VMEM((16, rows + 32, 128), F32),
+            pltpu.VMEM((2, rows + 16, 128), F32),
             pltpu.SemaphoreType.DMA((3, 3)),
         ],
     )(meta, fwd, adj, absn, near, far)
@@ -485,30 +503,32 @@
 
     cuts = sorted({a for a, _, _ in cover(own)} | {a for a, _, _ in cover(got)} | {out.shape[1]})
 
-    def piece(parts, a, b):
+    def piece(parts, a, b, i):
         for at, size, ref in cover(parts):
             if at <= a and b <= at + size:
-                return ref[0, a - at : b - at, :]
+                return ref[i, a - at : b - at, :]
 
     for a, b in zip(cuts[:-1], cuts[1:]):
-        shallow = pltpu.roll(packed[a:b, :], (128 - 8 * x) % 128, axis=1)
-        deep = piece(own, a, b) + piece(got, a, b)
-        out[0, a:b, :] = jnp.where(iota((b - a, 128), 1) < 4, shallow, deep)
+        for i in range(PLANES):
+            shift = (128 - 8 * (PLANES * x + i)) % 128
+            shallow = pltpu.roll(packed[a:b, :], shift, axis=1)
+            deep = piece(own, a, b, i) + piece(got, a, b, i)
+            out[i, a:b, :] = jnp.where(iota((b - a, 128), 1) < 4, shallow, deep)
 
 
 def final_call(own, got, keep, recv):
     half = keep.shape[1]
 
     def spec(a):
-        return pl.BlockSpec((1, a.shape[1], 128), lambda x: (x, 0, 0))
+        return pl.BlockSpec((PLANES, a.shape[1], 128), lambda x: (x, 0, 0))
 
     whole = pl.BlockSpec((64, half), lambda x: (0, 0))
     return pl.pallas_call(
         functools.partial(final_kernel, n_own=len(own), n_got=len(got)),
         out_shape=jax.ShapeDtypeStruct((8, half, 128), F32),
-        grid=(8,),
+        grid=(8 // PLANES,),
         in_specs=[spec(a) for a in own + got] + [whole, whole],
-        out_specs=pl.BlockSpec((1, half, 128), lambda x: (x, 0, 0)),
+        out_specs=pl.BlockSpec((PLANES, half, 128), lambda x: (x, 0, 0)),
         scratch_shapes=[pltpu.VMEM((half, 128), F32)],
         name="final",
     )(*own, *got, keep, recv)
@@ -548,15 +568,11 @@
         far = lax.ppermute(far, ALL, far_pairs)
         return near, far
 
-    out = faces_call(meta, fwd, adj, absorption, CHUNKS[0])
-    halos = [exchange(*out)]
-    meta = after(meta, *out)
-    out = pack_call(meta, fwd, adj, absorption, patterns, CHUNKS[1:])
-    t1, t2, src, near, far = out[-5:]
-    meta = after(meta, near, far)
-    near, far = exchange(near, far)
-    for c in range(1, len(CHUNKS)):
-        halos.append(exchange(*out[2 * c - 2 : 2 * c]))
+    out = head_call(meta, fwd, adj, absorption, patterns, CHUNKS)
+    t1, t2, src = out[-3:]
+    halos = [exchange(out[2 * c], out[2 * c + 1]) for c in range(len(CHUNKS))]
+    near, far = halos[0]
+    meta = after(meta, t1)
 
     def table(phase):
         angle = 2.0 * math.pi / total_x * (phase % total_x).astype(F32)
@@ -570,8 +586,9 @@
     to_data = jnp.concatenate(table(bins[None, :, None] * x_in[:, None, :]), axis=1)
     to_data = to_data.reshape(8 * 32, parts)
     from_data = jnp.concatenate(table(bins[:, None] * x_out[None, :]), axis=0)
-    seen = jnp.tile(after(measured, meta).reshape(32, 16), (1, 8))
-    meta = after(meta, to_data, from_data, seen)
+    seen = measured.reshape(32, 16)
+    meta = after(meta, to_data, from_data)
+    nh = halos[0][0].shape[1]
 
     own, arrived = [], []
 
@@ -585,25 +602,33 @@
 
     meta = deep(meta, 0)
     fsh, surf = vmem_call(
-        functools.partial(forward_kernel, ny=ny), [(8, 8, ny), (parts, 128)], shallow_scratch(ny), 5
+        functools.partial(forward_kernel, ny=ny),
+        [(8, 8, ny), (parts, 128)],
+        shallow_scratch(ny, nh),
+        3,
+        2,
     )(meta, t1, t2, src, near, far)
     meta = after(meta, surf)
     got = lax.all_to_all(surf, GX, 0, 0, tiled=True)
     meta = deep(meta, 1)
-    model, rows = vmem_call(data_kernel, [(32, 128), (parts, 256)], [], 4)(
+    model, rows = vmem_call(
+        data_kernel, [(32, 128), (parts, 256)], [pltpu.VMEM((32, 128), F32)], 4
+    )(
         meta, got, to_data, from_data, seen
     )
     meta = after(meta, rows)
     back = lax.all_to_all(rows, GX, 0, 0, tiled=True)
-    for c in range(2, len(CHUNKS)):
-        meta = deep(meta, c)
     send, keep = vmem_call(
         functools.partial(adjoint_kernel, ny=ny),
         [(64, ny // 2), (64, ny // 2)],
-        shallow_scratch(ny) + [pltpu.VMEM((64, ny), F32)],
-        6,
-    )(meta, t1, t2, back, near, far, fsh)
+        shallow_scratch(ny, nh) + [pltpu.VMEM((64, ny), F32)],
+        4,
+        2,
+    )(meta, t1, t2, back, fsh, near, far)
+    meta = after(meta, send)
     recv = lax.ppermute(send, ALL, pat_pairs)
+    for c in range(2, len(CHUNKS)):
+        meta = deep(meta, c)
     gradient = final_call(own, arrived, keep, recv)
     return (gradient, model[:, :16].reshape(1, 2, 16, 16))
 

time: 211 us -> 209 us (level)
  waiting for transfers between devices: 73.1 us -> 87.8 us
  Pallas kernels: 83.2 us -> 73.4 us
  starting transfers between devices: 42.7 us -> 36.4 us
    all_to_all x1, waiting for transfers between devices: 19.3 us -> 38.8 us  [shards(): got = lax.all_to_all(surf, GX, 0, 0, tiled=True)]
    ppermute x4 -> x3, starting transfers between devices: 23.2 us -> 17.1 us  [exchange(): far = lax.ppermute(far, ALL, far_pairs)]
    ppermute x1, waiting for transfers between devices: 5.2 us -> 0.01 us  [shards(): recv = lax.ppermute(send, ALL, pat_pairs)]
    pallas_call x3 -> x2, Pallas kernels: 19.5 us -> 14.3 us  [the longest x1 11.5 us: head_call(): pl.pallas_call(functools.partial(head_kernel, chunks=chunks, ny=ny), out_...]
    pallas_call x3, Pallas kernels: 47.2 us -> 42.7 us  [deep_call(): pl.pallas_call(functools.partial(deep_kernel, sends=sends, offset=offset,...]
    ppermute x4 -> x3, waiting for transfers between devices: 38.2 us -> 40.3 us  [exchange(): far = lax.ppermute(far, ALL, far_pairs)]
  transfers between devices with their start and end apart: 13 -> 11, of which waited for: 5 -> 4; matrix products, arithmetic and copies ran while one was open for 2% -> 2% of each run, Pallas kernels for 35% -> 28%
where the time goes in v2:
time: 209 us; the launch traced here: 206 us
  waiting for transfers between devices  87.8 us (42%)
  Pallas kernels  73.4 us (35%)
  starting transfers between devices  36.4 us (17%)
  local copies, waits for them, and re-layouts  4.8 us (2%)
  other arithmetic  2.14 us (1%)
    pallas_call x3, Pallas kernels, deep_call(): pl.pallas_call(functools.partial(deep_kernel, sends=sends, offset=offset,...  42.7 us
    ppermute x3, waiting for transfers between devices, exchange(): far = lax.ppermute(far, ALL, far_pairs)  40.3 us
    all_to_all x1, waiting for transfers between devices, shards(): got = lax.all_to_all(surf, GX, 0, 0, tiled=True)  38.8 us
    ppermute x3, starting transfers between devices, exchange(): far = lax.ppermute(far, ALL, far_pairs)  17.1 us
    pallas_call x1, Pallas kernels, head_call(): pl.pallas_call(functools.partial(head_kernel, chunks=chunks, ny=ny), out_...  11.5 us
    all_to_all x1, starting transfers between devices, shards(): got = lax.all_to_all(surf, GX, 0, 0, tiled=True)  10.3 us
    all_to_all x1, waiting for transfers between devices, shards(): back = lax.all_to_all(rows, GX, 0, 0, tiled=True)  8.57 us
    all_to_all x1, starting transfers between devices, shards(): back = lax.all_to_all(rows, GX, 0, 0, tiled=True)  6.02 us
  transfers between devices with their start and end apart: 11, of which 4 were waited for; matrix products, arithmetic and copies ran while one was open for 2% of the time, Pallas kernels for 28%

profile of v2, /device:TPU:32, one launch (start us, length us, event | category | flops | bytes accessed | tf_op | source)
XLA Modules:
  0.0 206.0 jit_solution(6930215285744163540)
XLA Ops:
  1.3 0.6 stack.27.meta
  1.9 11.5 %head.1 = (f32[14,272,128]{2,1,0:T(8,128)}, f32[14,272,128]{2,1,0:T(8,128)}, f32[11,272,128]{2,1,0:T(8,128)}, f32[11,272,128]{2,1,0:T(8,128)}, f32[11,520,128]{2...) custom-call(s32[5]{0:T(128)} %stack.27.meta, ...), custom_call_target="tpu_custom_call" | custom-call | tf_op jit(solution)/shard_map/head/pallas_call | solution.py:149
  13.4 0.1 collective-permute-start
  13.5 7.0 %collective-permute-start.1 = (f32[14,272,128]{2,1,0:T(8,128)}, f32[14,272,128]{2,1,0:T(8,128)}, u32[]{:S(2)}, u32[]{:S(2)}) collective-permute-start(f32[14,272,128]{2,1,0:T(8,128)} %get-tuple-element.30), channel_id=1, source_target_pairs={{1,2},{2,1},{3,4},{4,3},{5,6},{6,5},{7,8},{8,7},{9,10},{10,9},{11,... | collective-permute-start | bytes 5849096 | tf_op jit(solution)/shard_map/ppermute | solution.py:568
  20.5 0.1 collective-permute-start.4
  20.6 3.1 %collective-permute-start.5 = (f32[11,520,128]{2,1,0:T(8,128)}, f32[11,520,128]{2,1,0:T(8,128)}, u32[]{:S(2)}, u32[]{:S(2)}) collective-permute-start(f32[11,520,128]{2,1,0:T(8,128)} %get-tuple-element.45), channel_id=1, source_target_pairs={{1,2},{2,1},{3,4},{4,3},{5,6},{6,5},{7,8},{8,7},{9,10},{10,9},{11,... | collective-permute-start | bytes 8785928 | tf_op jit(solution)/shard_map/ppermute | solution.py:568
  23.7 0.1 collective-permute-start.2
  23.8 0.0 collective-permute-done.near.near_hbm
  23.8 0.0 copy-start
  23.8 7.0 %collective-permute-start.3 = (f32[11,272,128]{2,1,0:T(8,128)}, f32[11,272,128]{2,1,0:T(8,128)}, u32[]{:S(2)}, u32[]{:S(2)}) collective-permute-start(f32[11,272,128]{2,1,0:T(8,128)} %get-tuple-element.37), channel_id=1, source_target_pairs={{1,2},{2,1},{3,4},{4,3},{5,6},{6,5},{7,8},{8,7},{9,10},{10,9},{11,... | collective-permute-start | bytes 4595720 | tf_op jit(solution)/shard_map/ppermute | solution.py:568
  30.8 0.1 broadcast_add_fusion
  30.9 0.1 add.81
  31.0 0.0 copy-done.7
  31.0 0.3 cosine_multiply_fusion
  31.3 0.7 pad_maximum_fusion.1.back
  32.0 0.3 cosine_multiply_fusion.1
  32.4 0.7 pad_maximum_fusion
  33.1 11.0 %collective-permute-done.1.far.far_hbm = f32[14,272,128]{2,1,0:T(8,128)} collective-permute-done((f32[14,272,128]{2,1,0:T(8,128)}, f32[14,272,128]{2,1,0:T(8,128)}, u32[]{:S(2)}, u32[]{:S(2)}) %collective-permute-start.1) | collective-permute-done | bytes 1949728 | tf_op jit(solution)/shard_map/ppermute | solution.py:568
  44.1 12.7 %shard_map.86 = f32[8,256,128]{2,1,0:T(8,128)} custom-call(s32[5]{0:T(128)} %stack.27.meta, f32[8,1024,128]{2,1,0:T(8,128)} %bitcast.19, f32[8,1024,128]{2,1,0:T(8,128)} %bitcast.23, f32[8,1024,128]{2,1,0:T(8,128)} %absn.7, f32[14,272,128]{2,1,0:T(8,128)} %copy-done, f32[14,272,128]{2,1,0:T(8,128)} %collective-permute-done.1.far.far_hbm), custom_call_target="tpu_custom_call" | custom-call | tf_op jit(solution)/shard_map/pallas_call | solution.py:465
  56.8 5.8 %shard_map.87 = (f32[8,8,1024]{2,1,0:T(8,128)}, f32[64,128]{1,0:T(8,128)}) custom-call(s32[5]{0:T(128)} %stack.27.meta, f32[128,1024]{1,0:T(8,128)} %get-tuple-element.25.t1, f32[64,1024]{1,0:T(8,128)} %get-tuple-element.32.t2, f32[8,1024]{1,0:T(8,128)} %get-tuple-element.33.src, f32[14,272,128]{2,1,0:T(8,128)} %copy-done, ...), custom_call_target="tpu_custom_call" | custom-call | tf_op jit(solution)/shard_map/pallas_call | solution.py:604
  62.5 0.0 copy-start.2
  62.6 0.0 collective-permute-done.2.near
  62.6 29.3 %collective-permute-done.3.far = f32[11,272,128]{2,1,0:T(8,128)} collective-permute-done((f32[11,272,128]{2,1,0:T(8,128)}, f32[11,272,128]{2,1,0:T(8,128)}, u32[]{:S(2)}, u32[]{:S(2)}) %collective-permute-start.3) | collective-permute-done | bytes 1531936 | tf_op jit(solution)/shard_map/ppermute | solution.py:568
  91.9 0.0 copy-done.1
  91.9 12.7 %shard_map.88 = f32[8,256,128]{2,1,0:T(8,128)} custom-call(s32[5]{0:T(128)} %stack.27.meta, f32[8,1024,128]{2,1,0:T(8,128)} %bitcast.20, f32[8,1024,128]{2,1,0:T(8,128)} %bitcast.24, f32[8,1024,128]{2,1,0:T(8,128)} %absn.7, f32[11,272,128]{2,1,0:T(8,128)} %copy-done.1, f32[11,272,128]{2,1,0:T(8,128)} %collective-permute-done.3.far), custom_call_target="tpu_custom_call" | custom-call | tf_op jit(solution)/shard_map/pallas_call | solution.py:465
  104.6 1.6 collective-permute-start.7
  106.1 0.5 collective-permute-start.6
  106.7 10.3 %all-to-all-start = ((f32[64,1,128]{2,1,0:T(1,128)}), f32[64,1,128]{2,1,0:T(1,128)S(1)}, u32[]{:S(2)}, u32[]{:S(2)}) async-start(f32[64,1,128]{2,1,0:T(1,128)} %bitcast.8), calls=%async_computation | async-start | bytes 65536 | tf_op jit(solution)/shard_map/all_to_all | solution.py:612
  116.9 38.8 %all-to-all-done = f32[64,1,128]{2,1,0:T(1,128)S(1)} async-done(((f32[64,1,128]{2,1,0:T(1,128)}), f32[64,1,128]{2,1,0:T(1,128)S(1)}, u32[]{:S(2)}, u32[]{:S(2)}) %all-to-all-start) | async-done | bytes 32800 | tf_op jit(solution)/shard_map/all_to_all | solution.py:612
  155.8 0.6 copy-done.6
  156.4 2.8 %shard_map.89 = (f32[32,128]{1,0:T(8,128)}, f32[64,256]{1,0:T(8,128)}) custom-call(s32[5]{0:T(128)} %stack.27.meta, f32[64,128]{1,0:T(8,128)} %bitcast.28, f32[256,64]{1,0:T(8,128)} %bitcast.26, f32[32,1024]{1,0:T(8,128)} %pad_maximum_fusion.1.back, f32[32,16]{1,0:T(8,128)} %bitcast.30), custom_call_target="tpu_custom_call" | custom-call | tf_op jit(solution)/shard_map/pallas_call | solution.py:614
  159.2 1.5 copy.10
  160.8 6.0 %all-to-all-start.1 = ((f32[64,1,256]{2,1,0:T(1,128)}), f32[64,1,256]{2,1,0:T(1,128)S(1)}, u32[]{:S(2)}, u32[]{:S(2)}) async-start(f32[64,1,256]{2,1,0:T(1,128)} %copy.10), calls=%async_computation.1 | async-start | bytes 131072 | tf_op jit(solution)/shard_map/all_to_all | solution.py:620
  166.8 8.6 %all-to-all-done.1 = f32[64,1,256]{2,1,0:T(1,128)S(1)} async-done(((f32[64,1,256]{2,1,0:T(1,128)}), f32[64,1,256]{2,1,0:T(1,128)S(1)}, u32[]{:S(2)}, u32[]{:S(2)}) %all-to-all-start.1) | async-done | bytes 65568 | tf_op jit(solution)/shard_map/all_to_all | solution.py:620
  175.3 0.6 copy.13
  176.0 5.9 %shard_map.90 = (f32[64,512]{1,0:T(8,128)}, f32[64,512]{1,0:T(8,128)}) custom-call(s32[5]{0:T(128)} %stack.27.meta, f32[128,1024]{1,0:T(8,128)} %get-tuple-element.25.t1, f32[64,1024]{1,0:T(8,128)} %get-tuple-element.32.t2, f32[64,256]{1,0:T(8,128)} %bitcast.27, f32[8,8,1024]{2,1,0:T(8,128)} %get-tuple-element.41.fsh, f32[14,272,128]{2,1,0:T(8,128)} %copy-done, ...), custom_call_target="tpu_custom_call" | custom-call | tf_op jit(solution)/shard_map/pallas_call | solution.py:621
  181.9 0.6 collective-permute-start.8
  182.5 0.0 collective-permute-done.4.near
  182.5 0.0 collective-permute-done.5.far
  182.5 17.4 %shard_map.91.refs_0_ = f32[8,512,128]{2,1,0:T(8,128)} custom-call(s32[5]{0:T(128)} %stack.27.meta, f32[8,1024,128]{2,1,0:T(8,128)} %bitcast.21, f32[8,1024,128]{2,1,0:T(8,128)} %bitcast.25, f32[8,1024,128]{2,1,0:T(8,128)} %absn.7, f32[11,520,128]{2,1,0:T(8,128)} %collective-permute-done.4.near, f32[11,520,128]{2,1,0:T(8,128)} %collective-permute-done.5.far), custom_call_target="tpu_custom_call" | custom-call | tf_op jit(solution)/shard_map/pallas_call | solution.py:465
  199.8 0.0 collective-permute-done.8.refs_4_
  199.9 0.0 copy-start.5
  199.9 0.0 collective-permute-done.7.refs_2_
  199.9 0.0 collective-permute-done.6.refs_1_
  199.9 0.6 copy-done.5
  200.5 0.4 copy-done.3
  200.9 0.4 copy-done.4
  201.2 4.7 %final.1 = f32[8,512,128]{2,1,0:T(8,128)} custom-call(f32[8,512,128]{2,1,0:T(8,128)} %shard_map.91.refs_0_, f32[8,256,128]{2,1,0:T(8,128)} %copy-done.4, f32[8,256,128]{2,1,0:T(8,128)} %copy-done.3, f32[64,512]{1,0:T(8,128)} %get-tuple-element.46.refs_3_, f32[64,512]{1,0:T(8,128)} %copy-done.5), custom_call_target="tpu_custom_call" | custom-call | tf_op jit(solution)/shard_map/final/pallas_call | solution.py:526
  (10 shorter events, 0.0 us)
Async XLA Ops:
  1.9 29.1 %copy-start.7 = (s32[16]{0:T(128)S(1)}, s32[16]{0:T(128)}, u32[]{:S(2)}) copy-start(s32[16]{0:T(128)} %param.9) | copy-start | bytes 196
  13.4 10.4 %collective-permute-start = (f32[14,272,128]{2,1,0:T(8,128)}, f32[14,272,128]{2,1,0:T(8,128)S(1)}, u32[]{:S(2)}, u32[]{:S(2)}) collective-permute-start(f32[14,272,128]{2,1,0:T(8,128)} %get-tuple-element.29), channel_id=1, source_target_pairs={{0,1},{1,0},{2,3},{3,2},{4,5},{5,4},{6,7},{7,6},{8,9},{9,8},{10,11... | collective-permute-start | bytes 5849096 | tf_op jit(solution)/shard_map/ppermute | solution.py:567
  13.5 30.6 %collective-permute-start.1 = (f32[14,272,128]{2,1,0:T(8,128)}, f32[14,272,128]{2,1,0:T(8,128)}, u32[]{:S(2)}, u32[]{:S(2)}) collective-permute-start(f32[14,272,128]{2,1,0:T(8,128)} %get-tuple-element.30), channel_id=1, source_target_pairs={{1,2},{2,1},{3,4},{4,3},{5,6},{6,5},{7,8},{8,7},{9,10},{10,9},{11,... | collective-permute-start | bytes 5849096 | tf_op jit(solution)/shard_map/ppermute | solution.py:568
  20.5 162.0 %collective-permute-start.4 = (f32[11,520,128]{2,1,0:T(8,128)}, f32[11,520,128]{2,1,0:T(8,128)}, u32[]{:S(2)}, u32[]{:S(2)}) collective-permute-start(f32[11,520,128]{2,1,0:T(8,128)} %get-tuple-element.44), channel_id=1, source_target_pairs={{0,1},{1,0},{2,3},{3,2},{4,5},{5,4},{6,7},{7,6},{8,9},{9,8},{10,11... | collective-permute-start | bytes 8785928 | tf_op jit(solution)/shard_map/ppermute | solution.py:567
  20.6 161.9 %collective-permute-start.5 = (f32[11,520,128]{2,1,0:T(8,128)}, f32[11,520,128]{2,1,0:T(8,128)}, u32[]{:S(2)}, u32[]{:S(2)}) collective-permute-start(f32[11,520,128]{2,1,0:T(8,128)} %get-tuple-element.45), channel_id=1, source_target_pairs={{1,2},{2,1},{3,4},{4,3},{5,6},{6,5},{7,8},{8,7},{9,10},{10,9},{11,... | collective-permute-start | bytes 8785928 | tf_op jit(solution)/shard_map/ppermute | solution.py:568
  23.7 38.9 %collective-permute-start.2 = (f32[11,272,128]{2,1,0:T(8,128)}, f32[11,272,128]{2,1,0:T(8,128)S(1)}, u32[]{:S(2)}, u32[]{:S(2)}) collective-permute-start(f32[11,272,128]{2,1,0:T(8,128)} %get-tuple-element.36), channel_id=1, source_target_pairs={{0,1},{1,0},{2,3},{3,2},{4,5},{5,4},{6,7},{7,6},{8,9},{9,8},{10,11... | collective-permute-start | bytes 4595720 | tf_op jit(solution)/shard_map/ppermute | solution.py:567
  23.8 20.3 %copy-start = (f32[14,272,128]{2,1,0:T(8,128)}, f32[14,272,128]{2,1,0:T(8,128)S(1)}, u32[]{:S(2)}) copy-start(f32[14,272,128]{2,1,0:T(8,128)S(1)} %collective-permute-done.near.near_hbm) | copy-start | bytes 5849092
  23.8 68.1 %collective-permute-start.3 = (f32[11,272,128]{2,1,0:T(8,128)}, f32[11,272,128]{2,1,0:T(8,128)}, u32[]{:S(2)}, u32[]{:S(2)}) collective-permute-start(f32[11,272,128]{2,1,0:T(8,128)} %get-tuple-element.37), channel_id=1, source_target_pairs={{1,2},{2,1},{3,4},{4,3},{5,6},{6,5},{7,8},{8,7},{9,10},{10,9},{11,... | collective-permute-start | bytes 4595720 | tf_op jit(solution)/shard_map/ppermute | solution.py:568
  62.5 43.6 %copy-start.2 = (f32[8,256,128]{2,1,0:T(8,128)S(1)}, f32[8,256,128]{2,1,0:T(8,128)}, u32[]{:S(2)}) copy-start(f32[8,256,128]{2,1,0:T(8,128)} %shard_map.86) | copy-start | bytes 3145732
  62.6 29.3 %copy-start.1 = (f32[11,272,128]{2,1,0:T(8,128)}, f32[11,272,128]{2,1,0:T(8,128)S(1)}, u32[]{:S(2)}) copy-start(f32[11,272,128]{2,1,0:T(8,128)S(1)} %collective-permute-done.2.near) | copy-start | bytes 4595716
  104.6 95.3 %collective-permute-start.7 = (f32[8,256,128]{2,1,0:T(8,128)}, f32[8,256,128]{2,1,0:T(8,128)S(1)}, u32[]{:S(2)}, u32[]{:S(2)}) collective-permute-start(f32[8,256,128]{2,1,0:T(8,128)} %shard_map.88), channel_id=1, source_target_pairs={{0,64},{1,65},{2,66},{3,67},{4,68},{5,69},{6,70},{7,71},{8,72},{9,... | collective-permute-start | bytes 3145736 | tf_op jit(solution)/shard_map/ppermute | solution.py:598
  106.1 93.8 %collective-permute-start.6 = (f32[8,256,128]{2,1,0:T(8,128)S(1)}, f32[8,256,128]{2,1,0:T(8,128)S(1)}, u32[]{:S(2)}, u32[]{:S(2)}) collective-permute-start(f32[8,256,128]{2,1,0:T(8,128)S(1)} %copy-done.2), channel_id=1, source_target_pairs={{0,64},{1,65},{2,66},{3,67},{4,68},{5,69},{6,70},{7,71},{8,72},{9,... | collective-permute-start | bytes 3145736 | tf_op jit(solution)/shard_map/ppermute | solution.py:598
  106.7 49.1 %all-to-all-start = ((f32[64,1,128]{2,1,0:T(1,128)}), f32[64,1,128]{2,1,0:T(1,128)S(1)}, u32[]{:S(2)}, u32[]{:S(2)}) async-start(f32[64,1,128]{2,1,0:T(1,128)} %bitcast.8), calls=%async_computation | async-start | bytes 65536 | tf_op jit(solution)/shard_map/all_to_all | solution.py:612
  155.8 0.6 copy-start.6
  160.8 14.6 %all-to-all-start.1 = ((f32[64,1,256]{2,1,0:T(1,128)}), f32[64,1,256]{2,1,0:T(1,128)S(1)}, u32[]{:S(2)}, u32[]{:S(2)}) async-start(f32[64,1,256]{2,1,0:T(1,128)} %copy.10), calls=%async_computation.1 | async-start | bytes 131072 | tf_op jit(solution)/shard_map/all_to_all | solution.py:620
  181.9 18.0 %collective-permute-start.8 = (f32[64,512]{1,0:T(8,128)}, f32[64,512]{1,0:T(8,128)S(1)}, u32[]{:S(2)}, u32[]{:S(2)}) collective-permute-start(f32[64,512]{1,0:T(8,128)} %get-tuple-element.42), channel_id=1, source_target_pairs={{0,64},{1,65},{2,66},{3,67},{4,68},{5,69},{6,70},{7,71},{8,72},{9,... | collective-permute-start | bytes 393224 | tf_op jit(solution)/shard_map/ppermute | solution.py:629
  199.9 0.6 copy-start.5
  199.9 1.0 copy-start.3
  199.9 1.3 copy-start.4

commit v3 on v2

--- a/solution.py
+++ b/solution.py
@@ -64,10 +64,10 @@
     return at // nh, at % nh
 
 
-def head_kernel(meta, fwd, adj, absn, pats, *rest, chunks, ny):
-    n = 2 * len(chunks)
-    faces = rest[:n]
-    t1, t2, src, fs, ad, ab, near, far, in_sem, src_sem, face_sem, sh_sem = rest[n:]
+def head_kernel(
+    meta, fwd, adj, absn, pats, face0, face1, t1, t2, src, near, far, fs, ad, ab,
+    in_sem, src_sem, face_sem, *, chunk, ny
+):
     loads = []
     for i, (h, v) in enumerate(((fwd, fs), (adj, ad), (absn, ab))):
         cp = pltpu.make_async_copy(h, v, in_sem.at[i])
@@ -90,14 +90,10 @@
     loads[1].wait()
     pack(ad, t1, 64)
     loads[2].wait()
-    outs = []
-    for c, chunk in enumerate(chunks):
-        outs += face_copies(
-            meta, (fs, ad, ab), 0, faces[2 * c], faces[2 * c + 1], face_sem.at[c], chunk, ny
-        )
+    outs = face_copies(meta, (fs, ad, ab), 0, face0, face1, face_sem, chunk, ny)
     pack(ab, t2, 0)
     src_cp.wait()
-    nh = halo_rows(chunks[0][2], ny)
+    nh = near.shape[1]
 
     def put(dst, value, row):
         for v in range(ny // 128):
@@ -130,34 +126,27 @@
         low_face(near)
         high_face(far)
 
-    for i, (v, h) in enumerate(((near, faces[0]), (far, faces[1]))):
-        cp = pltpu.make_async_copy(v, h.at[pl.ds(11, 3)], sh_sem.at[i])
-        cp.start()
-        outs.append(cp)
     for cp in outs:
         cp.wait()
 
 
-def head_call(meta, fwd, adj, absn, pats, chunks):
+def head_call(meta, fwd, adj, absn, pats, chunk):
     ny = fwd.shape[1]
-    small = [(128, ny), (64, ny), (8, ny)]
-    shapes = []
-    for c, (_, _, rows) in enumerate(chunks):
-        shapes += [(11 if c else 14, halo_rows(rows, ny), 128)] * 2
+    face = (11, halo_rows(chunk[2], ny), 128)
+    shallow = (3, SHALLOW_ROWS * ny // 128 // 3, 128)
+    shapes = [face, face, (128, ny), (64, ny), (8, ny), shallow, shallow]
     any_spec = pl.BlockSpec(memory_space=pl.ANY)
     vmem = pl.BlockSpec(memory_space=pltpu.VMEM)
     return pl.pallas_call(
-        functools.partial(head_kernel, chunks=chunks, ny=ny),
-        out_shape=[jax.ShapeDtypeStruct(s, F32) for s in shapes + small],
+        functools.partial(head_kernel, chunk=chunk, ny=ny),
+        out_shape=[jax.ShapeDtypeStruct(s, F32) for s in shapes],
         in_specs=[pl.BlockSpec(memory_space=pltpu.SMEM)] + [any_spec] * 4,
-        out_specs=[any_spec] * len(shapes) + [vmem] * 3,
+        out_specs=[any_spec] * 2 + [vmem] * 5,
         scratch_shapes=[pltpu.VMEM((8, ny, 128), F32)] * 3
-        + [pltpu.VMEM((3, shapes[0][1], 128), F32)] * 2
         + [
             pltpu.SemaphoreType.DMA((3,)),
             pltpu.SemaphoreType.DMA(()),
-            pltpu.SemaphoreType.DMA((len(chunks), 2, 3)),
-            pltpu.SemaphoreType.DMA((2,)),
+            pltpu.SemaphoreType.DMA((2, 3)),
         ],
         name="head",
     )(meta, fwd, adj, absn, pats)
@@ -186,17 +175,7 @@
     return jnp.where(core0, b, a), jnp.where(core0, a, b)
 
 
-def fetch_shallow(near_hbm, far_hbm, near, far, sem):
-    cps = []
-    for i, (h, v) in enumerate(((near_hbm, near), (far_hbm, far))):
-        cp = pltpu.make_async_copy(h.at[pl.ds(11, 3)], v, sem.at[i])
-        cp.start()
-        cps.append(cp)
-    for cp in cps:
-        cp.wait()
-
-
-def shallow_solve(meta, start, at, near, far, near_at, t2, f0, f1, r, s, ny):
+def shallow_solve(meta, start, at, near, far, near_at, t2, f0, f1, r, s, ny, midway=None):
     lo_ok = jnp.where(meta[1] > 0, 1.0, 0.0).astype(F32)
     hi_ok = jnp.where(meta[2] > 0, 1.0, 0.0).astype(F32)
     core0 = meta[4] == 0
@@ -219,6 +198,8 @@
     for k in range(SWEEPS):
         w = sweep_weight(k)
         old, new = bufs[k % 2], bufs[1 - k % 2]
+        if k == 2 and midway is not None:
+            midway()
 
         def pair(q, carry, old=old, new=new, w=w, k=k):
             p = k + 1 + 2 * q
@@ -236,10 +217,27 @@
         lax.fori_loop(0, 7 - k, pair, 0)
 
 
-def forward_kernel(
-    meta, t1, t2, src, near_hbm, far_hbm, fsh, surf, near, far, sem, f0, f1, r, s, *, ny
-):
-    fetch_shallow(near_hbm, far_hbm, near, far, sem)
+def forward_kernel(meta, t1, t2, src, near, far, fwd, adj, absn, fsh, surf, *rest, chunks, ny):
+    n = 2 * len(chunks)
+    faces = rest[:n]
+    f0, f1, r, s, fs, ad, ab, in_sem, face_sem = rest[n:]
+    loads = []
+    for i, (h, v) in enumerate(((fwd, fs), (adj, ad), (absn, ab))):
+        cp = pltpu.make_async_copy(h, v, in_sem.at[i])
+        cp.start()
+        loads.append(cp)
+    outs = []
+
+    def midway():
+        for cp in loads:
+            cp.wait()
+        for c, chunk in enumerate(chunks):
+            outs.extend(
+                face_copies(
+                    meta, (fs, ad, ab), 0, faces[2 * c], faces[2 * c + 1], face_sem.at[c], chunk, ny
+                )
+            )
+
     z0 = iota((8, ny), 0) == 0
     lo, hi = shallow_side(near, far, meta[4] == 0, 88, ny)
     for i in range(3):
@@ -247,20 +245,37 @@
         s[12 + i] = jnp.where(z0, hi[i : i + 1, :], 0.0)
     for i in range(8):
         s[4 + i] = jnp.where(z0, src[i : i + 1, :], 0.0)
-    shallow_solve(meta, t1, 0, near, far, 0, t2, f0, f1, r, s, ny)
+    shallow_solve(meta, t1, 0, near, far, 0, t2, f0, f1, r, s, ny, midway)
     for i in range(8):
         fsh[i] = f0[4 + i]
     top = jnp.concatenate([f0[4 + i, 0:1, :] for i in range(8)], axis=0)
     for v in range(ny // 128):
         surf[8 * v : 8 * v + 8, :] = group_transpose(top[:, 128 * v : 128 * v + 128])
-
-
-def shallow_scratch(ny, nh):
-    return (
-        [pltpu.VMEM((3, nh, 128), F32)] * 2
-        + [pltpu.SemaphoreType.DMA((2,))]
-        + [pltpu.VMEM((16, 8, ny), F32)] * 4
-    )
+    for cp in outs:
+        cp.wait()
+
+
+def forward_call(meta, t1, t2, src, near, far, fwd, adj, absn, chunks):
+    ny = fwd.shape[1]
+    any_spec = pl.BlockSpec(memory_space=pl.ANY)
+    vmem = pl.BlockSpec(memory_space=pltpu.VMEM)
+    shapes = [(8, 8, ny), (ny // 16, 128)]
+    for _, _, rows in chunks:
+        shapes += [(11, halo_rows(rows, ny), 128)] * 2
+    return pl.pallas_call(
+        functools.partial(forward_kernel, chunks=chunks, ny=ny),
+        out_shape=[jax.ShapeDtypeStruct(s, F32) for s in shapes],
+        in_specs=[pl.BlockSpec(memory_space=pltpu.SMEM)] + [vmem] * 5 + [any_spec] * 3,
+        out_specs=[vmem] * 2 + [any_spec] * (2 * len(chunks)),
+        scratch_shapes=shallow_scratch(ny)
+        + [pltpu.VMEM((8, ny, 128), F32)] * 3
+        + [pltpu.SemaphoreType.DMA((3,)), pltpu.SemaphoreType.DMA((len(chunks), 2, 3))],
+        name="shallow_forward",
+    )(meta, t1, t2, src, near, far, fwd, adj, absn)
+
+
+def shallow_scratch(ny):
+    return [pltpu.VMEM((16, 8, ny), F32)] * 4
 
 
 def vmem_call(kernel, out_shapes, scratch, n_in, n_any=0):
@@ -276,9 +291,8 @@
 
 
 def adjoint_kernel(
-    meta, t1, t2, got, fsh, near_hbm, far_hbm, send, keep, near, far, sem, f0, f1, r, s, prod, *, ny
+    meta, t1, t2, got, near, far, fsh, send, keep, f0, f1, r, s, prod, *, ny
 ):
-    fetch_shallow(near_hbm, far_hbm, near, far, sem)
     z0 = iota((8, ny), 0) == 0
     for h in range(2):
         parts = []
@@ -568,10 +582,10 @@
         far = lax.ppermute(far, ALL, far_pairs)
         return near, far
 
-    out = head_call(meta, fwd, adj, absorption, patterns, CHUNKS)
-    t1, t2, src = out[-3:]
-    halos = [exchange(out[2 * c], out[2 * c + 1]) for c in range(len(CHUNKS))]
-    near, far = halos[0]
+    out = head_call(meta, fwd, adj, absorption, patterns, CHUNKS[0])
+    t1, t2, src = out[2:5]
+    near, far = exchange(out[5], out[6])
+    halos = [exchange(out[0], out[1])]
     meta = after(meta, t1)
 
     def table(phase):
@@ -588,7 +602,6 @@
     from_data = jnp.concatenate(table(bins[:, None] * x_out[None, :]), axis=0)
     seen = measured.reshape(32, 16)
     meta = after(meta, to_data, from_data)
-    nh = halos[0][0].shape[1]
 
     own, arrived = [], []
 
@@ -600,31 +613,24 @@
             own.append(terms)
         return after(meta, terms)
 
-    meta = deep(meta, 0)
-    fsh, surf = vmem_call(
-        functools.partial(forward_kernel, ny=ny),
-        [(8, 8, ny), (parts, 128)],
-        shallow_scratch(ny, nh),
-        3,
-        2,
-    )(meta, t1, t2, src, near, far)
+    fsh, surf, *faces = forward_call(meta, t1, t2, src, near, far, fwd, adj, absorption, CHUNKS[1:])
     meta = after(meta, surf)
     got = lax.all_to_all(surf, GX, 0, 0, tiled=True)
-    meta = deep(meta, 1)
+    for c in range(1, len(CHUNKS)):
+        halos.append(exchange(faces[2 * c - 2], faces[2 * c - 1]))
     model, rows = vmem_call(
         data_kernel, [(32, 128), (parts, 256)], [pltpu.VMEM((32, 128), F32)], 4
-    )(
-        meta, got, to_data, from_data, seen
-    )
+    )(meta, got, to_data, from_data, seen)
     meta = after(meta, rows)
     back = lax.all_to_all(rows, GX, 0, 0, tiled=True)
+    meta = deep(meta, 0)
+    meta = deep(meta, 1)
     send, keep = vmem_call(
         functools.partial(adjoint_kernel, ny=ny),
         [(64, ny // 2), (64, ny // 2)],
-        shallow_scratch(ny, nh) + [pltpu.VMEM((64, ny), F32)],
-        4,
-        2,
-    )(meta, t1, t2, back, fsh, near, far)
+        shallow_scratch(ny) + [pltpu.VMEM((64, ny), F32)],
+        6,
+    )(meta, t1, t2, back, near, far, fsh)
     meta = after(meta, send)
     recv = lax.ppermute(send, ALL, pat_pairs)
     for c in range(2, len(CHUNKS)):

time: 209 us -> 215 us (1.029)
  blocking collectives: 0 us -> 39.4 us
  waiting for transfers between devices: 87.8 us -> 55.7 us
  starting transfers between devices: 36.4 us -> 34.1 us
    all_to_all x0 -> x1, blocking collectives: none -> 39.4 us  [shards(): back = lax.all_to_all(rows, GX, 0, 0, tiled=True)]
    ppermute x3 -> x4, waiting for transfers between devices: 40.3 us -> 4.47 us  [exchange(): far = lax.ppermute(far, ALL, far_pairs)]
    all_to_all x1, waiting for transfers between devices: 38.8 us -> 51.2 us  [shards(): got = lax.all_to_all(surf, GX, 0, 0, tiled=True)]
    all_to_all x1 -> x0, waiting for transfers between devices: 8.57 us -> none  [shards(): back = lax.all_to_all(rows, GX, 0, 0, tiled=True)]
    ppermute x3 -> x4, starting transfers between devices: 17.1 us -> 24.1 us  [exchange(): far = lax.ppermute(far, ALL, far_pairs)]
    all_to_all x1 -> x0, starting transfers between devices: 6.02 us -> none  [shards(): back = lax.all_to_all(rows, GX, 0, 0, tiled=True)]
    all_to_all x1, starting transfers between devices: 10.3 us -> 7.27 us  [shards(): got = lax.all_to_all(surf, GX, 0, 0, tiled=True)]
  transfers between devices with their start and end apart: 11 -> 12, of which waited for: 4 -> 2; matrix products, arithmetic and copies ran while one was open for 2% -> 1% of each run, Pallas kernels for 28% -> 29%
where the time goes in v3:
time: 215 us; the launch traced here: 212 us
  Pallas kernels  74.2 us (35%)
  waiting for transfers between devices  55.7 us (26%)
  blocking collectives  39.4 us (18%)
  starting transfers between devices  34.1 us (16%)
  local copies, waits for them, and re-layouts  4.98 us (2%)
    all_to_all x1, waiting for transfers between devices, shards(): got = lax.all_to_all(surf, GX, 0, 0, tiled=True)  51.2 us
    pallas_call x3, Pallas kernels, deep_call(): pl.pallas_call(functools.partial(deep_kernel, sends=sends, offset=offset,...  42.7 us
    all_to_all x1, blocking collectives, shards(): back = lax.all_to_all(rows, GX, 0, 0, tiled=True)  39.4 us
    ppermute x4, starting transfers between devices, exchange(): far = lax.ppermute(far, ALL, far_pairs)  24.1 us
    pallas_call x1, Pallas kernels, forward_call(): pl.pallas_call(functools.partial(forward_kernel, chunks=chunks, ny=ny), o...  10.3 us
    pallas_call x1, Pallas kernels, head_call(): pl.pallas_call(functools.partial(head_kernel, chunk=chunk, ny=ny), out_sh...  8.59 us
    all_to_all x1, starting transfers between devices, shards(): got = lax.all_to_all(surf, GX, 0, 0, tiled=True)  7.27 us
    pallas_call x1, Pallas kernels, shards(): vmem_call(functools.partial(adjoint_kernel, ny=ny), [(64, ny // 2), (64,...  4.95 us
  transfers between devices with their start and end apart: 12, of which 2 were waited for; matrix products, arithmetic and copies ran while one was open for 1% of the time, Pallas kernels for 29%

profile of v3, /device:TPU:32, one launch (start us, length us, event | category | flops | bytes accessed | tf_op | source)
XLA Modules:
  0.0 212.1 jit_solution(2951364795650458521)
XLA Ops:
  1.3 0.6 stack.27.meta
  1.9 8.6 %head.1 = (f32[11,272,128]{2,1,0:T(8,128)}, f32[11,272,128]{2,1,0:T(8,128)}, f32[128,1024]{1,0:T(8,128)}, f32[64,1024]{1,0:T(8,128)}, f32[8,1024]{1,0:T(8,128)},...) custom-call(s32[5]{0:T(128)} %stack.27.meta, f32[8,1024,128]{2,1,0:T(8,128)} %bitcast.18, f32[8,1024,128]{2,1,0:T(8,128)} %bitcast.23, ...), custom_call_target="tpu_custom_call" | custom-call | tf_op jit(solution)/shard_map/head/pallas_call | solution.py:140
  10.5 0.1 collective-permute-start
  10.6 7.0 %collective-permute-start.1 = (f32[3,256,128]{2,1,0:T(8,128)}, f32[3,256,128]{2,1,0:T(8,128)S(1)}, u32[]{:S(2)}, u32[]{:S(2)}) collective-permute-start(f32[3,256,128]{2,1,0:T(8,128)} %get-tuple-element.34), channel_id=1, source_target_pairs={{1,2},{2,1},{3,4},{4,3},{5,6},{6,5},{7,8},{8,7},{9,10},{10,9},{11,... | collective-permute-start | bytes 1179656 | tf_op jit(solution)/shard_map/ppermute | solution.py:582
  17.6 0.1 collective-permute-start.2
  17.7 0.1 broadcast_add_fusion
  17.8 0.1 add.81
  17.9 0.3 cosine_multiply_fusion
  18.2 0.7 pad_maximum_fusion.1.back
  18.9 0.3 cosine_multiply_fusion.1
  19.2 0.7 pad_maximum_fusion
  19.9 0.0 collective-permute-done.near
  19.9 4.5 %collective-permute-done.1.far = f32[3,256,128]{2,1,0:T(8,128)S(1)} collective-permute-done((f32[3,256,128]{2,1,0:T(8,128)}, f32[3,256,128]{2,1,0:T(8,128)S(1)}, u32[]{:S(2)}, u32[]{:S(2)}) %collective-permute-start.1) | collective-permute-done | bytes 393248 | tf_op jit(solution)/shard_map/ppermute | solution.py:582
  24.4 0.7 copy-done.2
  25.1 10.3 %shallow_forward.1 = (f32[8,8,1024]{2,1,0:T(8,128)}, f32[64,128]{1,0:T(8,128)}, f32[11,272,128]{2,1,0:T(8,128)}, f32[11,272,128]{2,1,0:T(8,128)}, f32[11,520,128]{2,1,0:T(8,128)}, /*index=5*/f32[11,520,128]{2,1,0:T(8,128)}) custom-call(s32[5]{0:T(128)} %stack.27.meta, f32[128,1024]{1,0:T(8,128)} %get-tuple-element.27.t1, f32[64,1024]{1,0:T(8,128)} %get-tuple-element.31.t2, ...), custom_call_target="tpu_custom_call" | custom-call | tf_op jit(solution)/shard_map/shallow_forward/pallas_call | solution.py:265
  35.5 0.1 collective-permute-start.6
  35.6 7.0 %collective-permute-start.7 = (f32[11,520,128]{2,1,0:T(8,128)}, f32[11,520,128]{2,1,0:T(8,128)}, u32[]{:S(2)}, u32[]{:S(2)}) collective-permute-start(f32[11,520,128]{2,1,0:T(8,128)} %get-tuple-element.49), channel_id=1, source_target_pairs={{1,2},{2,1},{3,4},{4,3},{5,6},{6,5},{7,8},{8,7},{9,10},{10,9},{11,... | collective-permute-start | bytes 8785928 | tf_op jit(solution)/shard_map/ppermute | solution.py:582
  42.6 3.1 %collective-permute-start.3 = (f32[11,272,128]{2,1,0:T(8,128)}, f32[11,272,128]{2,1,0:T(8,128)}, u32[]{:S(2)}, u32[]{:S(2)}) collective-permute-start(f32[11,272,128]{2,1,0:T(8,128)} %get-tuple-element.40), channel_id=1, source_target_pairs={{1,2},{2,1},{3,4},{4,3},{5,6},{6,5},{7,8},{8,7},{9,10},{10,9},{11,... | collective-permute-start | bytes 4595720 | tf_op jit(solution)/shard_map/ppermute | solution.py:582
  45.7 0.1 collective-permute-start.4
  45.8 0.0 collective-permute-done.2.near
  45.8 7.0 %collective-permute-start.5 = (f32[11,272,128]{2,1,0:T(8,128)}, f32[11,272,128]{2,1,0:T(8,128)}, u32[]{:S(2)}, u32[]{:S(2)}) collective-permute-start(f32[11,272,128]{2,1,0:T(8,128)} %get-tuple-element.43), channel_id=1, source_target_pairs={{1,2},{2,1},{3,4},{4,3},{5,6},{6,5},{7,8},{8,7},{9,10},{10,9},{11,... | collective-permute-start | bytes 4595720 | tf_op jit(solution)/shard_map/ppermute | solution.py:582
  52.8 7.3 %all-to-all-start = ((f32[64,1,128]{2,1,0:T(1,128)}), f32[64,1,128]{2,1,0:T(1,128)S(1)}, u32[]{:S(2)}, u32[]{:S(2)}) async-start(f32[64,1,128]{2,1,0:T(1,128)} %bitcast.32), calls=%async_computation | async-start | bytes 65536 | tf_op jit(solution)/shard_map/all_to_all | solution.py:618
  60.1 51.2 %all-to-all-done = f32[64,1,128]{2,1,0:T(1,128)S(1)} async-done(((f32[64,1,128]{2,1,0:T(1,128)}), f32[64,1,128]{2,1,0:T(1,128)S(1)}, u32[]{:S(2)}, u32[]{:S(2)}) %all-to-all-start) | async-done | bytes 32800 | tf_op jit(solution)/shard_map/all_to_all | solution.py:618
  111.3 0.6 copy-done.4
  112.0 2.8 %shard_map.86 = (f32[32,128]{1,0:T(8,128)}, f32[64,256]{1,0:T(8,128)}) custom-call(s32[5]{0:T(128)} %stack.27.meta, f32[64,128]{1,0:T(8,128)} %bitcast.30, f32[256,64]{1,0:T(8,128)} %bitcast.28, f32[32,1024]{1,0:T(8,128)} %pad_maximum_fusion.1.back, f32[32,16]{1,0:T(8,128)} %bitcast.33), custom_call_target="tpu_custom_call" | custom-call | tf_op jit(solution)/shard_map/pallas_call | solution.py:621
  114.8 0.0 collective-permute-done.3.far
  114.8 12.7 %shard_map.87 = f32[8,256,128]{2,1,0:T(8,128)} custom-call(s32[5]{0:T(128)} %stack.27.meta, f32[8,1024,128]{2,1,0:T(8,128)} %bitcast.20, f32[8,1024,128]{2,1,0:T(8,128)} %bitcast.25, f32[8,1024,128]{2,1,0:T(8,128)} %absn.9, f32[11,272,128]{2,1,0:T(8,128)} %collective-permute-done.2.near, f32[11,272,128]{2,1,0:T(8,128)} %collective-permute-done.3.far), custom_call_target="tpu_custom_call" | custom-call | tf_op jit(solution)/shard_map/pallas_call | solution.py:479
  127.5 0.0 copy-start.5
  127.5 1.6 collective-permute-start.8
  129.1 0.0 collective-permute-done.4.near
  129.1 0.0 collective-permute-done.5.far
  129.1 12.7 %shard_map.88 = f32[8,256,128]{2,1,0:T(8,128)} custom-call(s32[5]{0:T(128)} %stack.27.meta, f32[8,1024,128]{2,1,0:T(8,128)} %bitcast.21, f32[8,1024,128]{2,1,0:T(8,128)} %bitcast.26, f32[8,1024,128]{2,1,0:T(8,128)} %absn.9, f32[11,272,128]{2,1,0:T(8,128)} %collective-permute-done.4.near, f32[11,272,128]{2,1,0:T(8,128)} %collective-permute-done.5.far), custom_call_target="tpu_custom_call" | custom-call | tf_op jit(solution)/shard_map/pallas_call | solution.py:479
  141.8 0.5 collective-permute-start.9
  142.3 0.0 copy-done.5
  142.4 0.1 copy.10
  142.4 39.4 %all_to_all.22 = f32[64,1,256]{2,1,0:T(1,128)S(1)} all-to-all(f32[64,1,256]{2,1,0:T(1,128)S(1)} %copy.10), channel_id=1, replica_groups=mesh['pat'=2,'gx_0'=4,'gx_1'=2,'gx_2'=4,'gx_3'=2] {'gx_0','gx_1','gx_2',..., dimensions={0} | all-to-all | bytes 131072 | tf_op jit(solution)/shard_map/all_to_all | solution.py:625
  181.9 0.6 copy.13
  182.5 4.9 %shard_map.89 = (f32[64,512]{1,0:T(8,128)}, f32[64,512]{1,0:T(8,128)}) custom-call(s32[5]{0:T(128)} %stack.27.meta, f32[128,1024]{1,0:T(8,128)} %get-tuple-element.27.t1, f32[64,1024]{1,0:T(8,128)} %get-tuple-element.31.t2, f32[64,256]{1,0:T(8,128)} %bitcast.29, f32[3,256,128]{2,1,0:T(8,128)} %copy-done.1, f32[3,256,128]{2,1,0:T(8,128)} %copy-done.2, ...), custom_call_target="tpu_custom_call" | custom-call | tf_op jit(solution)/shard_map/pallas_call | solution.py:628
  187.4 0.2 collective-permute-start.10
  187.7 0.0 collective-permute-done.6.near
  187.7 0.0 collective-permute-done.7.far
  187.7 1.6 copy-done
  189.3 17.4 %shard_map.90.refs_0_ = f32[8,512,128]{2,1,0:T(8,128)} custom-call(s32[5]{0:T(128)} %stack.27.meta, f32[8,1024,128]{2,1,0:T(8,128)} %bitcast.22, f32[8,1024,128]{2,1,0:T(8,128)} %bitcast.27, f32[8,1024,128]{2,1,0:T(8,128)} %absn.9, f32[11,520,128]{2,1,0:T(8,128)} %copy-done, f32[11,520,128]{2,1,0:T(8,128)} %collective-permute-done.7.far), custom_call_target="tpu_custom_call" | custom-call | tf_op jit(solution)/shard_map/pallas_call | solution.py:479
  206.7 0.0 collective-permute-done.10.refs_4_
  206.7 0.0 collective-permute-done.8.refs_1_
  206.7 0.0 collective-permute-done.9.refs_2_
  206.7 0.6 copy-done.3
  207.3 4.7 %final.1 = f32[8,512,128]{2,1,0:T(8,128)} custom-call(f32[8,512,128]{2,1,0:T(8,128)} %shard_map.90.refs_0_, f32[8,256,128]{2,1,0:T(8,128)} %collective-permute-done.8.refs_1_, f32[8,256,128]{2,1,0:T(8,128)} %collective-permute-done.9.refs_2_, f32[64,512]{1,0:T(8,128)} %get-tuple-element.50.refs_3_, f32[64,512]{1,0:T(8,128)} %copy-done.3), custom_call_target="tpu_custom_call" | custom-call | tf_op jit(solution)/shard_map/final/pallas_call | solution.py:540
  (11 shorter events, 0.0 us)
Async XLA Ops:
  1.9 16.0 %copy-start.6 = (s32[16]{0:T(128)S(1)}, s32[16]{0:T(128)}, u32[]{:S(2)}) copy-start(s32[16]{0:T(128)} %param.9) | copy-start | bytes 196
  10.5 9.4 %collective-permute-start = (f32[3,256,128]{2,1,0:T(8,128)}, f32[3,256,128]{2,1,0:T(8,128)S(1)}, u32[]{:S(2)}, u32[]{:S(2)}) collective-permute-start(f32[3,256,128]{2,1,0:T(8,128)} %get-tuple-element.33), channel_id=1, source_target_pairs={{0,1},{1,0},{2,3},{3,2},{4,5},{5,4},{6,7},{7,6},{8,9},{9,8},{10,11... | collective-permute-start | bytes 1179656 | tf_op jit(solution)/shard_map/ppermute | solution.py:581
  10.6 13.8 %collective-permute-start.1 = (f32[3,256,128]{2,1,0:T(8,128)}, f32[3,256,128]{2,1,0:T(8,128)S(1)}, u32[]{:S(2)}, u32[]{:S(2)}) collective-permute-start(f32[3,256,128]{2,1,0:T(8,128)} %get-tuple-element.34), channel_id=1, source_target_pairs={{1,2},{2,1},{3,4},{4,3},{5,6},{6,5},{7,8},{8,7},{9,10},{10,9},{11,... | collective-permute-start | bytes 1179656 | tf_op jit(solution)/shard_map/ppermute | solution.py:582
  17.6 28.2 %collective-permute-start.2 = (f32[11,272,128]{2,1,0:T(8,128)}, f32[11,272,128]{2,1,0:T(8,128)}, u32[]{:S(2)}, u32[]{:S(2)}) collective-permute-start(f32[11,272,128]{2,1,0:T(8,128)} %get-tuple-element.39), channel_id=1, source_target_pairs={{0,1},{1,0},{2,3},{3,2},{4,5},{5,4},{6,7},{7,6},{8,9},{9,8},{10,11... | collective-permute-start | bytes 4595720 | tf_op jit(solution)/shard_map/ppermute | solution.py:581
  19.9 4.5 %copy-start.1 = (f32[3,256,128]{2,1,0:T(8,128)}, f32[3,256,128]{2,1,0:T(8,128)S(1)}, u32[]{:S(2)}) copy-start(f32[3,256,128]{2,1,0:T(8,128)S(1)} %collective-permute-done.near) | copy-start | bytes 1179652
  24.4 0.7 copy-start.2
  35.5 152.2 %collective-permute-start.6 = (f32[11,520,128]{2,1,0:T(8,128)}, f32[11,520,128]{2,1,0:T(8,128)S(1)}, u32[]{:S(2)}, u32[]{:S(2)}) collective-permute-start(f32[11,520,128]{2,1,0:T(8,128)} %get-tuple-element.48), channel_id=1, source_target_pairs={{0,1},{1,0},{2,3},{3,2},{4,5},{5,4},{6,7},{7,6},{8,9},{9,8},{10,11... | collective-permute-start | bytes 8785928 | tf_op jit(solution)/shard_map/ppermute | solution.py:581
  35.6 152.1 %collective-permute-start.7 = (f32[11,520,128]{2,1,0:T(8,128)}, f32[11,520,128]{2,1,0:T(8,128)}, u32[]{:S(2)}, u32[]{:S(2)}) collective-permute-start(f32[11,520,128]{2,1,0:T(8,128)} %get-tuple-element.49), channel_id=1, source_target_pairs={{1,2},{2,1},{3,4},{4,3},{5,6},{6,5},{7,8},{8,7},{9,10},{10,9},{11,... | collective-permute-start | bytes 8785928 | tf_op jit(solution)/shard_map/ppermute | solution.py:582
  42.6 72.2 %collective-permute-start.3 = (f32[11,272,128]{2,1,0:T(8,128)}, f32[11,272,128]{2,1,0:T(8,128)}, u32[]{:S(2)}, u32[]{:S(2)}) collective-permute-start(f32[11,272,128]{2,1,0:T(8,128)} %get-tuple-element.40), channel_id=1, source_target_pairs={{1,2},{2,1},{3,4},{4,3},{5,6},{6,5},{7,8},{8,7},{9,10},{10,9},{11,... | collective-permute-start | bytes 4595720 | tf_op jit(solution)/shard_map/ppermute | solution.py:582
  45.7 83.4 %collective-permute-start.4 = (f32[11,272,128]{2,1,0:T(8,128)}, f32[11,272,128]{2,1,0:T(8,128)}, u32[]{:S(2)}, u32[]{:S(2)}) collective-permute-start(f32[11,272,128]{2,1,0:T(8,128)} %get-tuple-element.42), channel_id=1, source_target_pairs={{0,1},{1,0},{2,3},{3,2},{4,5},{5,4},{6,7},{7,6},{8,9},{9,8},{10,11... | collective-permute-start | bytes 4595720 | tf_op jit(solution)/shard_map/ppermute | solution.py:581
  45.8 83.3 %collective-permute-start.5 = (f32[11,272,128]{2,1,0:T(8,128)}, f32[11,272,128]{2,1,0:T(8,128)}, u32[]{:S(2)}, u32[]{:S(2)}) collective-permute-start(f32[11,272,128]{2,1,0:T(8,128)} %get-tuple-element.43), channel_id=1, source_target_pairs={{1,2},{2,1},{3,4},{4,3},{5,6},{6,5},{7,8},{8,7},{9,10},{10,9},{11,... | collective-permute-start | bytes 4595720 | tf_op jit(solution)/shard_map/ppermute | solution.py:582
  52.8 58.5 %all-to-all-start = ((f32[64,1,128]{2,1,0:T(1,128)}), f32[64,1,128]{2,1,0:T(1,128)S(1)}, u32[]{:S(2)}, u32[]{:S(2)}) async-start(f32[64,1,128]{2,1,0:T(1,128)} %bitcast.32), calls=%async_computation | async-start | bytes 65536 | tf_op jit(solution)/shard_map/all_to_all | solution.py:618
  111.3 0.6 copy-start.4
  127.5 14.9 %copy-start.5 = (f32[64,256]{1,0:T(8,128)S(1)}, f32[64,256]{1,0:T(8,128)}, u32[]{:S(2)}) copy-start(f32[64,256]{1,0:T(8,128)} %get-tuple-element.37) | copy-start | bytes 196612
  127.5 79.2 %collective-permute-start.8 = (f32[8,256,128]{2,1,0:T(8,128)}, f32[8,256,128]{2,1,0:T(8,128)}, u32[]{:S(2)}, u32[]{:S(2)}) collective-permute-start(f32[8,256,128]{2,1,0:T(8,128)} %shard_map.87), channel_id=1, source_target_pairs={{0,64},{1,65},{2,66},{3,67},{4,68},{5,69},{6,70},{7,71},{8,72},{9,... | collective-permute-start | bytes 3145736 | tf_op jit(solution)/shard_map/ppermute | solution.py:611
  141.8 64.9 %collective-permute-start.9 = (f32[8,256,128]{2,1,0:T(8,128)}, f32[8,256,128]{2,1,0:T(8,128)}, u32[]{:S(2)}, u32[]{:S(2)}) collective-permute-start(f32[8,256,128]{2,1,0:T(8,128)} %shard_map.88), channel_id=1, source_target_pairs={{0,64},{1,65},{2,66},{3,67},{4,68},{5,69},{6,70},{7,71},{8,72},{9,... | collective-permute-start | bytes 3145736 | tf_op jit(solution)/shard_map/ppermute | solution.py:611
  187.4 19.2 %collective-permute-start.10 = (f32[64,512]{1,0:T(8,128)}, f32[64,512]{1,0:T(8,128)S(1)}, u32[]{:S(2)}, u32[]{:S(2)}) collective-permute-start(f32[64,512]{1,0:T(8,128)} %get-tuple-element.46), channel_id=1, source_target_pairs={{0,64},{1,65},{2,66},{3,67},{4,68},{5,69},{6,70},{7,71},{8,72},{9,... | collective-permute-start | bytes 393224 | tf_op jit(solution)/shard_map/ppermute | solution.py:635
  187.7 1.6 copy-start
  206.7 0.6 copy-start.3

commit v4 on v3

--- a/solution.py
+++ b/solution.py
@@ -18,6 +18,7 @@
 BF16 = jnp.bfloat16
 MXU_PLANES = (1,)
 PLANES = 2
+EARLY = 2
 
 
 def sweep_weight(sweep):
@@ -65,9 +66,11 @@
 
 
 def head_kernel(
-    meta, fwd, adj, absn, pats, face0, face1, t1, t2, src, near, far, fs, ad, ab,
-    in_sem, src_sem, face_sem, *, chunk, ny
+    meta, fwd, adj, absn, pats, *rest, chunks, ny
 ):
+    n = 2 * len(chunks)
+    faces = rest[:n]
+    t1, t2, src, near, far, fs, ad, ab, in_sem, src_sem, face_sem = rest[n:]
     loads = []
     for i, (h, v) in enumerate(((fwd, fs), (adj, ad), (absn, ab))):
         cp = pltpu.make_async_copy(h, v, in_sem.at[i])
@@ -90,7 +93,11 @@
     loads[1].wait()
     pack(ad, t1, 64)
     loads[2].wait()
-    outs = face_copies(meta, (fs, ad, ab), 0, face0, face1, face_sem, chunk, ny)
+    outs = []
+    for c, chunk in enumerate(chunks):
+        outs += face_copies(
+            meta, (fs, ad, ab), 0, faces[2 * c], faces[2 * c + 1], face_sem.at[c], chunk, ny
+        )
     pack(ab, t2, 0)
     src_cp.wait()
     nh = near.shape[1]
@@ -130,23 +137,25 @@
         cp.wait()
 
 
-def head_call(meta, fwd, adj, absn, pats, chunk):
+def head_call(meta, fwd, adj, absn, pats, chunks):
     ny = fwd.shape[1]
-    face = (11, halo_rows(chunk[2], ny), 128)
     shallow = (3, SHALLOW_ROWS * ny // 128 // 3, 128)
-    shapes = [face, face, (128, ny), (64, ny), (8, ny), shallow, shallow]
+    shapes = []
+    for _, _, rows in chunks:
+        shapes += [(11, halo_rows(rows, ny), 128)] * 2
+    shapes += [(128, ny), (64, ny), (8, ny), shallow, shallow]
     any_spec = pl.BlockSpec(memory_space=pl.ANY)
     vmem = pl.BlockSpec(memory_space=pltpu.VMEM)
     return pl.pallas_call(
-        functools.partial(head_kernel, chunk=chunk, ny=ny),
+        functools.partial(head_kernel, chunks=chunks, ny=ny),
         out_shape=[jax.ShapeDtypeStruct(s, F32) for s in shapes],
         in_specs=[pl.BlockSpec(memory_space=pltpu.SMEM)] + [any_spec] * 4,
-        out_specs=[any_spec] * 2 + [vmem] * 5,
+        out_specs=[any_spec] * (2 * len(chunks)) + [vmem] * 5,
         scratch_shapes=[pltpu.VMEM((8, ny, 128), F32)] * 3
         + [
             pltpu.SemaphoreType.DMA((3,)),
             pltpu.SemaphoreType.DMA(()),
-            pltpu.SemaphoreType.DMA((2, 3)),
+            pltpu.SemaphoreType.DMA((len(chunks), 2, 3)),
         ],
         name="head",
     )(meta, fwd, adj, absn, pats)
@@ -582,10 +591,10 @@
         far = lax.ppermute(far, ALL, far_pairs)
         return near, far
 
-    out = head_call(meta, fwd, adj, absorption, patterns, CHUNKS[0])
-    t1, t2, src = out[2:5]
-    near, far = exchange(out[5], out[6])
-    halos = [exchange(out[0], out[1])]
+    out = head_call(meta, fwd, adj, absorption, patterns, CHUNKS[:EARLY])
+    t1, t2, src, near, far = out[2 * EARLY :]
+    near, far = exchange(near, far)
+    halos = [exchange(out[2 * c], out[2 * c + 1]) for c in range(EARLY)]
     meta = after(meta, t1)
 
     def table(phase):
@@ -613,28 +622,29 @@
             own.append(terms)
         return after(meta, terms)
 
-    fsh, surf, *faces = forward_call(meta, t1, t2, src, near, far, fwd, adj, absorption, CHUNKS[1:])
+    fsh, surf, *faces = forward_call(
+        meta, t1, t2, src, near, far, fwd, adj, absorption, CHUNKS[EARLY:]
+    )
     meta = after(meta, surf)
     got = lax.all_to_all(surf, GX, 0, 0, tiled=True)
-    for c in range(1, len(CHUNKS)):
-        halos.append(exchange(faces[2 * c - 2], faces[2 * c - 1]))
+    for c in range(EARLY, len(CHUNKS)):
+        at = 2 * (c - EARLY)
+        halos.append(exchange(faces[at], faces[at + 1]))
+    meta = deep(meta, 0)
     model, rows = vmem_call(
         data_kernel, [(32, 128), (parts, 256)], [pltpu.VMEM((32, 128), F32)], 4
     )(meta, got, to_data, from_data, seen)
     meta = after(meta, rows)
     back = lax.all_to_all(rows, GX, 0, 0, tiled=True)
-    meta = deep(meta, 0)
-    meta = deep(meta, 1)
+    for c in range(1, len(CHUNKS)):
+        meta = deep(meta, c)
     send, keep = vmem_call(
         functools.partial(adjoint_kernel, ny=ny),
         [(64, ny // 2), (64, ny // 2)],
         shallow_scratch(ny) + [pltpu.VMEM((64, ny), F32)],
         6,
     )(meta, t1, t2, back, near, far, fsh)
-    meta = after(meta, send)
     recv = lax.ppermute(send, ALL, pat_pairs)
-    for c in range(2, len(CHUNKS)):
-        meta = deep(meta, c)
     gradient = final_call(own, arrived, keep, recv)
     return (gradient, model[:, :16].reshape(1, 2, 16, 16))
 

time: 215 us -> 220 us (1.023)
  blocking collectives: 39.4 us -> 0 us
  waiting for transfers between devices: 55.7 us -> 90 us
  starting transfers between devices: 34.1 us -> 44.2 us
    all_to_all x1, waiting for transfers between devices: 51.2 us -> 5.3 us  [shards(): got = lax.all_to_all(surf, GX, 0, 0, tiled=True)]
    all_to_all x0 -> x1, waiting for transfers between devices: none -> 41.4 us  [shards(): back = lax.all_to_all(rows, GX, 0, 0, tiled=True)]
    all_to_all x1 -> x0, blocking collectives: 39.4 us -> none  [shards(): back = lax.all_to_all(rows, GX, 0, 0, tiled=True)]
    ppermute x4, waiting for transfers between devices: 4.47 us -> 37.8 us  [exchange(): far = lax.ppermute(far, ALL, far_pairs)]
    all_to_all x0 -> x1, starting transfers between devices: none -> 10.2 us  [shards(): back = lax.all_to_all(rows, GX, 0, 0, tiled=True)]
    ppermute x1, waiting for transfers between devices: 0.01 us -> 5.51 us  [shards(): recv = lax.ppermute(send, ALL, pat_pairs)]
  transfers between devices with their start and end apart: 12 -> 13, of which waited for: 2 -> 5; matrix products, arithmetic and copies ran while one was open for 1% -> 2% of each run, Pallas kernels for 29% -> 28%
where the time goes in v4:
time: 220 us; the launch traced here: 218 us
  waiting for transfers between devices  90 us (41%)
  Pallas kernels  74.4 us (34%)
  starting transfers between devices  44.2 us (20%)
  local copies, waits for them, and re-layouts  5.61 us (3%)
    pallas_call x3, Pallas kernels, deep_call(): pl.pallas_call(functools.partial(deep_kernel, sends=sends, offset=offset,...  42.8 us
    all_to_all x1, waiting for transfers between devices, shards(): back = lax.all_to_all(rows, GX, 0, 0, tiled=True)  41.4 us
    ppermute x4, waiting for transfers between devices, exchange(): far = lax.ppermute(far, ALL, far_pairs)  37.8 us
    ppermute x4, starting transfers between devices, exchange(): far = lax.ppermute(far, ALL, far_pairs)  24.1 us
    all_to_all x1, starting transfers between devices, shards(): back = lax.all_to_all(rows, GX, 0, 0, tiled=True)  10.2 us
    pallas_call x1, Pallas kernels, head_call(): pl.pallas_call(functools.partial(head_kernel, chunks=chunks, ny=ny), out_...  9.67 us
    pallas_call x1, Pallas kernels, forward_call(): pl.pallas_call(functools.partial(forward_kernel, chunks=chunks, ny=ny), o...  9.36 us
    all_to_all x1, starting transfers between devices, shards(): got = lax.all_to_all(surf, GX, 0, 0, tiled=True)  7.27 us
  transfers between devices with their start and end apart: 13, of which 5 were waited for; matrix products, arithmetic and copies ran while one was open for 2% of the time, Pallas kernels for 28%

profile of v4, /device:TPU:32, one launch (start us, length us, event | category | flops | bytes accessed | tf_op | source)
XLA Modules:
  0.0 217.8 jit_solution(9659837867832424251)
XLA Ops:
  1.3 0.6 stack.27.meta
  1.9 9.7 %head.1 = (f32[11,272,128]{2,1,0:T(8,128)}, f32[11,272,128]{2,1,0:T(8,128)}, f32[11,272,128]{2,1,0:T(8,128)}, f32[11,272,128]{2,1,0:T(8,128)}, f32[128,1024]{1,0...) custom-call(s32[5]{0:T(128)} %stack.27.meta, ...), custom_call_target="tpu_custom_call" | custom-call | tf_op jit(solution)/shard_map/head/pallas_call | solution.py:149
  11.6 0.1 collective-permute-start
  11.7 7.0 %collective-permute-start.1 = (f32[3,256,128]{2,1,0:T(8,128)}, f32[3,256,128]{2,1,0:T(8,128)S(1)}, u32[]{:S(2)}, u32[]{:S(2)}) collective-permute-start(f32[3,256,128]{2,1,0:T(8,128)} %get-tuple-element.34), channel_id=1, source_target_pairs={{1,2},{2,1},{3,4},{4,3},{5,6},{6,5},{7,8},{8,7},{9,10},{10,9},{11,... | collective-permute-start | bytes 1179656 | tf_op jit(solution)/shard_map/ppermute | solution.py:591
  18.7 0.1 collective-permute-start.2
  18.8 0.1 broadcast_add_fusion
  18.9 0.1 add.81
  19.0 0.0 copy-done.6
  19.0 0.3 cosine_multiply_fusion
  19.3 0.7 pad_maximum_fusion.1.back
  20.0 0.3 cosine_multiply_fusion.1
  20.3 0.7 pad_maximum_fusion
  21.0 0.0 collective-permute-done.near
  21.0 4.5 %collective-permute-done.1.far = f32[3,256,128]{2,1,0:T(8,128)S(1)} collective-permute-done((f32[3,256,128]{2,1,0:T(8,128)}, f32[3,256,128]{2,1,0:T(8,128)S(1)}, u32[]{:S(2)}, u32[]{:S(2)}) %collective-permute-start.1) | collective-permute-done | bytes 393248 | tf_op jit(solution)/shard_map/ppermute | solution.py:591
  25.5 0.8 copy-done.2
  26.2 9.4 %shallow_forward.1 = (f32[8,8,1024]{2,1,0:T(8,128)}, f32[64,128]{1,0:T(8,128)}, f32[11,520,128]{2,1,0:T(8,128)}, f32[11,520,128]{2,1,0:T(8,128)}) custom-call(s32[5]{0:T(128)} %stack.27.meta, f32[128,1024]{1,0:T(8,128)} %get-tuple-element.27.t1, f32[64,1024]{1,0:T(8,128)} %get-tuple-element.31.t2, f32[8,1024]{1,0:T(8,128)} %get-tuple-element.32.src, ...), custom_call_target="tpu_custom_call" | custom-call | tf_op jit(solution)/shard_map/shallow_forward/pallas_call | solution.py:274
  35.6 0.1 collective-permute-start.6
  35.7 7.0 %collective-permute-start.7 = (f32[11,520,128]{2,1,0:T(8,128)}, f32[11,520,128]{2,1,0:T(8,128)}, u32[]{:S(2)}, u32[]{:S(2)}) collective-permute-start(f32[11,520,128]{2,1,0:T(8,128)} %get-tuple-element.46), channel_id=1, source_target_pairs={{1,2},{2,1},{3,4},{4,3},{5,6},{6,5},{7,8},{8,7},{9,10},{10,9},{11,... | collective-permute-start | bytes 8785928 | tf_op jit(solution)/shard_map/ppermute | solution.py:591
  42.7 3.1 %collective-permute-start.3 = (f32[11,272,128]{2,1,0:T(8,128)}, f32[11,272,128]{2,1,0:T(8,128)}, u32[]{:S(2)}, u32[]{:S(2)}) collective-permute-start(f32[11,272,128]{2,1,0:T(8,128)} %get-tuple-element.38), channel_id=1, source_target_pairs={{1,2},{2,1},{3,4},{4,3},{5,6},{6,5},{7,8},{8,7},{9,10},{10,9},{11,... | collective-permute-start | bytes 4595720 | tf_op jit(solution)/shard_map/ppermute | solution.py:591
  45.8 0.1 collective-permute-start.4
  45.9 0.0 collective-permute-done.2.near
  45.9 7.0 %collective-permute-start.5 = (f32[11,272,128]{2,1,0:T(8,128)}, f32[11,272,128]{2,1,0:T(8,128)}, u32[]{:S(2)}, u32[]{:S(2)}) collective-permute-start(f32[11,272,128]{2,1,0:T(8,128)} %get-tuple-element.43), channel_id=1, source_target_pairs={{1,2},{2,1},{3,4},{4,3},{5,6},{6,5},{7,8},{8,7},{9,10},{10,9},{11,... | collective-permute-start | bytes 4595720 | tf_op jit(solution)/shard_map/ppermute | solution.py:591
  52.9 7.3 %all-to-all-start = ((f32[64,1,128]{2,1,0:T(1,128)}), f32[64,1,128]{2,1,0:T(1,128)S(1)}, u32[]{:S(2)}, u32[]{:S(2)}) async-start(f32[64,1,128]{2,1,0:T(1,128)} %bitcast.32), calls=%async_computation | async-start | bytes 65536 | tf_op jit(solution)/shard_map/all_to_all | solution.py:629
  60.2 33.3 %collective-permute-done.3.far = f32[11,272,128]{2,1,0:T(8,128)} collective-permute-done((f32[11,272,128]{2,1,0:T(8,128)}, f32[11,272,128]{2,1,0:T(8,128)}, u32[]{:S(2)}, u32[]{:S(2)}) %collective-permute-start.3) | collective-permute-done | bytes 1531936 | tf_op jit(solution)/shard_map/ppermute | solution.py:591
  93.5 12.7 %shard_map.86 = f32[8,256,128]{2,1,0:T(8,128)} custom-call(s32[5]{0:T(128)} %stack.27.meta, f32[8,1024,128]{2,1,0:T(8,128)} %bitcast.20, f32[8,1024,128]{2,1,0:T(8,128)} %bitcast.25, f32[8,1024,128]{2,1,0:T(8,128)} %absn.9, f32[11,272,128]{2,1,0:T(8,128)} %collective-permute-done.2.near, f32[11,272,128]{2,1,0:T(8,128)} %collective-permute-done.3.far), custom_call_target="tpu_custom_call" | custom-call | tf_op jit(solution)/shard_map/pallas_call | solution.py:488
  106.2 5.3 %all-to-all-done = f32[64,1,128]{2,1,0:T(1,128)S(1)} async-done(((f32[64,1,128]{2,1,0:T(1,128)}), f32[64,1,128]{2,1,0:T(1,128)S(1)}, u32[]{:S(2)}, u32[]{:S(2)}) %all-to-all-start) | async-done | bytes 32800 | tf_op jit(solution)/shard_map/all_to_all | solution.py:629
  111.5 0.6 copy-done.4
  112.1 2.8 %shard_map.87 = (f32[32,128]{1,0:T(8,128)}, f32[64,256]{1,0:T(8,128)}) custom-call(s32[5]{0:T(128)} %stack.27.meta, f32[64,128]{1,0:T(8,128)} %bitcast.30, f32[256,64]{1,0:T(8,128)} %bitcast.28, f32[32,1024]{1,0:T(8,128)} %pad_maximum_fusion.1.back, f32[32,16]{1,0:T(8,128)} %bitcast.33), custom_call_target="tpu_custom_call" | custom-call | tf_op jit(solution)/shard_map/pallas_call | solution.py:634
  114.9 0.0 collective-permute-done.4.near
  114.9 0.0 collective-permute-done.5.far
  114.9 12.8 %shard_map.88 = f32[8,256,128]{2,1,0:T(8,128)} custom-call(s32[5]{0:T(128)} %stack.27.meta, f32[8,1024,128]{2,1,0:T(8,128)} %bitcast.21, f32[8,1024,128]{2,1,0:T(8,128)} %bitcast.26, f32[8,1024,128]{2,1,0:T(8,128)} %absn.9, f32[11,272,128]{2,1,0:T(8,128)} %collective-permute-done.4.near, f32[11,272,128]{2,1,0:T(8,128)} %collective-permute-done.5.far), custom_call_target="tpu_custom_call" | custom-call | tf_op jit(solution)/shard_map/pallas_call | solution.py:488
  127.7 1.7 collective-permute-start.9
  129.4 0.5 collective-permute-start.8
  129.8 0.7 copy.10
  130.5 10.2 %all-to-all-start.1 = ((f32[64,1,256]{2,1,0:T(1,128)}), f32[64,1,256]{2,1,0:T(1,128)S(1)}, u32[]{:S(2)}, u32[]{:S(2)}) async-start(f32[64,1,256]{2,1,0:T(1,128)} %copy.10), calls=%async_computation.1 | async-start | bytes 131072 | tf_op jit(solution)/shard_map/all_to_all | solution.py:638
  140.7 41.4 %all-to-all-done.1 = f32[64,1,256]{2,1,0:T(1,128)S(1)} async-done(((f32[64,1,256]{2,1,0:T(1,128)}), f32[64,1,256]{2,1,0:T(1,128)S(1)}, u32[]{:S(2)}, u32[]{:S(2)}) %all-to-all-start.1) | async-done | bytes 65568 | tf_op jit(solution)/shard_map/all_to_all | solution.py:638
  182.1 0.6 copy.13
  182.7 0.0 collective-permute-done.6.near
  182.7 0.0 collective-permute-done.7.far
  182.7 1.6 copy-done
  184.3 17.3 %shard_map.89.refs_0_ = f32[8,512,128]{2,1,0:T(8,128)} custom-call(s32[5]{0:T(128)} %stack.27.meta, f32[8,1024,128]{2,1,0:T(8,128)} %bitcast.22, f32[8,1024,128]{2,1,0:T(8,128)} %bitcast.27, f32[8,1024,128]{2,1,0:T(8,128)} %absn.9, f32[11,520,128]{2,1,0:T(8,128)} %copy-done, f32[11,520,128]{2,1,0:T(8,128)} %collective-permute-done.7.far), custom_call_target="tpu_custom_call" | custom-call | tf_op jit(solution)/shard_map/pallas_call | solution.py:488
  201.7 4.9 %shard_map.90 = (f32[64,512]{1,0:T(8,128)}, f32[64,512]{1,0:T(8,128)}) custom-call(s32[5]{0:T(128)} %stack.27.meta, f32[128,1024]{1,0:T(8,128)} %get-tuple-element.27.t1, f32[64,1024]{1,0:T(8,128)} %get-tuple-element.31.t2, f32[64,256]{1,0:T(8,128)} %bitcast.29, f32[3,256,128]{2,1,0:T(8,128)} %copy-done.1, f32[3,256,128]{2,1,0:T(8,128)} %copy-done.2, ...), custom_call_target="tpu_custom_call" | custom-call | tf_op jit(solution)/shard_map/pallas_call | solution.py:641
  206.6 0.2 collective-permute-start.10
  206.9 0.0 collective-permute-done.9.refs_2_
  206.9 0.0 collective-permute-done.8.refs_1_
  206.9 5.5 %collective-permute-done.10.refs_4_ = f32[64,512]{1,0:T(8,128)S(1)} collective-permute-done((f32[64,512]{1,0:T(8,128)}, f32[64,512]{1,0:T(8,128)S(1)}, u32[]{:S(2)}, u32[]{:S(2)}) %collective-permute-start.10) | collective-permute-done | bytes 131104 | tf_op jit(solution)/shard_map/ppermute | solution.py:647
  212.4 0.7 copy-done.3
  213.0 4.7 %final.1 = f32[8,512,128]{2,1,0:T(8,128)} custom-call(f32[8,512,128]{2,1,0:T(8,128)} %shard_map.89.refs_0_, f32[8,256,128]{2,1,0:T(8,128)} %collective-permute-done.8.refs_1_, f32[8,256,128]{2,1,0:T(8,128)} %collective-permute-done.9.refs_2_, f32[64,512]{1,0:T(8,128)} %get-tuple-element.49.refs_3_, f32[64,512]{1,0:T(8,128)} %copy-done.3), custom_call_target="tpu_custom_call" | custom-call | tf_op jit(solution)/shard_map/final/pallas_call | solution.py:549
  (12 shorter events, 0.0 us)
Async XLA Ops:
  1.9 17.1 %copy-start.6 = (s32[16]{0:T(128)S(1)}, s32[16]{0:T(128)}, u32[]{:S(2)}) copy-start(s32[16]{0:T(128)} %param.9) | copy-start | bytes 196
  11.6 9.4 %collective-permute-start = (f32[3,256,128]{2,1,0:T(8,128)}, f32[3,256,128]{2,1,0:T(8,128)S(1)}, u32[]{:S(2)}, u32[]{:S(2)}) collective-permute-start(f32[3,256,128]{2,1,0:T(8,128)} %get-tuple-element.33), channel_id=1, source_target_pairs={{0,1},{1,0},{2,3},{3,2},{4,5},{5,4},{6,7},{7,6},{8,9},{9,8},{10,11... | collective-permute-start | bytes 1179656 | tf_op jit(solution)/shard_map/ppermute | solution.py:590
  11.7 13.8 %collective-permute-start.1 = (f32[3,256,128]{2,1,0:T(8,128)}, f32[3,256,128]{2,1,0:T(8,128)S(1)}, u32[]{:S(2)}, u32[]{:S(2)}) collective-permute-start(f32[3,256,128]{2,1,0:T(8,128)} %get-tuple-element.34), channel_id=1, source_target_pairs={{1,2},{2,1},{3,4},{4,3},{5,6},{6,5},{7,8},{8,7},{9,10},{10,9},{11,... | collective-permute-start | bytes 1179656 | tf_op jit(solution)/shard_map/ppermute | solution.py:591
  18.7 27.2 %collective-permute-start.2 = (f32[11,272,128]{2,1,0:T(8,128)}, f32[11,272,128]{2,1,0:T(8,128)}, u32[]{:S(2)}, u32[]{:S(2)}) collective-permute-start(f32[11,272,128]{2,1,0:T(8,128)} %get-tuple-element.37), channel_id=1, source_target_pairs={{0,1},{1,0},{2,3},{3,2},{4,5},{5,4},{6,7},{7,6},{8,9},{9,8},{10,11... | collective-permute-start | bytes 4595720 | tf_op jit(solution)/shard_map/ppermute | solution.py:590
  21.0 4.5 %copy-start.1 = (f32[3,256,128]{2,1,0:T(8,128)}, f32[3,256,128]{2,1,0:T(8,128)S(1)}, u32[]{:S(2)}) copy-start(f32[3,256,128]{2,1,0:T(8,128)S(1)} %collective-permute-done.near) | copy-start | bytes 1179652
  25.5 0.8 copy-start.2
  35.6 147.1 %collective-permute-start.6 = (f32[11,520,128]{2,1,0:T(8,128)}, f32[11,520,128]{2,1,0:T(8,128)S(1)}, u32[]{:S(2)}, u32[]{:S(2)}) collective-permute-start(f32[11,520,128]{2,1,0:T(8,128)} %get-tuple-element.45), channel_id=1, source_target_pairs={{0,1},{1,0},{2,3},{3,2},{4,5},{5,4},{6,7},{7,6},{8,9},{9,8},{10,11... | collective-permute-start | bytes 8785928 | tf_op jit(solution)/shard_map/ppermute | solution.py:590
  35.7 147.0 %collective-permute-start.7 = (f32[11,520,128]{2,1,0:T(8,128)}, f32[11,520,128]{2,1,0:T(8,128)}, u32[]{:S(2)}, u32[]{:S(2)}) collective-permute-start(f32[11,520,128]{2,1,0:T(8,128)} %get-tuple-element.46), channel_id=1, source_target_pairs={{1,2},{2,1},{3,4},{4,3},{5,6},{6,5},{7,8},{8,7},{9,10},{10,9},{11,... | collective-permute-start | bytes 8785928 | tf_op jit(solution)/shard_map/ppermute | solution.py:591
  42.7 50.7 %collective-permute-start.3 = (f32[11,272,128]{2,1,0:T(8,128)}, f32[11,272,128]{2,1,0:T(8,128)}, u32[]{:S(2)}, u32[]{:S(2)}) collective-permute-start(f32[11,272,128]{2,1,0:T(8,128)} %get-tuple-element.38), channel_id=1, source_target_pairs={{1,2},{2,1},{3,4},{4,3},{5,6},{6,5},{7,8},{8,7},{9,10},{10,9},{11,... | collective-permute-start | bytes 4595720 | tf_op jit(solution)/shard_map/ppermute | solution.py:591
  45.8 69.1 %collective-permute-start.4 = (f32[11,272,128]{2,1,0:T(8,128)}, f32[11,272,128]{2,1,0:T(8,128)}, u32[]{:S(2)}, u32[]{:S(2)}) collective-permute-start(f32[11,272,128]{2,1,0:T(8,128)} %get-tuple-element.42), channel_id=1, source_target_pairs={{0,1},{1,0},{2,3},{3,2},{4,5},{5,4},{6,7},{7,6},{8,9},{9,8},{10,11... | collective-permute-start | bytes 4595720 | tf_op jit(solution)/shard_map/ppermute | solution.py:590
  45.9 69.0 %collective-permute-start.5 = (f32[11,272,128]{2,1,0:T(8,128)}, f32[11,272,128]{2,1,0:T(8,128)}, u32[]{:S(2)}, u32[]{:S(2)}) collective-permute-start(f32[11,272,128]{2,1,0:T(8,128)} %get-tuple-element.43), channel_id=1, source_target_pairs={{1,2},{2,1},{3,4},{4,3},{5,6},{6,5},{7,8},{8,7},{9,10},{10,9},{11,... | collective-permute-start | bytes 4595720 | tf_op jit(solution)/shard_map/ppermute | solution.py:591
  52.9 58.5 %all-to-all-start = ((f32[64,1,128]{2,1,0:T(1,128)}), f32[64,1,128]{2,1,0:T(1,128)S(1)}, u32[]{:S(2)}, u32[]{:S(2)}) async-start(f32[64,1,128]{2,1,0:T(1,128)} %bitcast.32), calls=%async_computation | async-start | bytes 65536 | tf_op jit(solution)/shard_map/all_to_all | solution.py:629
  111.5 0.6 copy-start.4
  114.9 14.9 %copy-start.5 = (f32[64,256]{1,0:T(8,128)S(1)}, f32[64,256]{1,0:T(8,128)}, u32[]{:S(2)}) copy-start(f32[64,256]{1,0:T(8,128)} %get-tuple-element.40) | copy-start | bytes 196612
  127.7 79.1 %collective-permute-start.9 = (f32[8,256,128]{2,1,0:T(8,128)}, f32[8,256,128]{2,1,0:T(8,128)}, u32[]{:S(2)}, u32[]{:S(2)}) collective-permute-start(f32[8,256,128]{2,1,0:T(8,128)} %shard_map.88), channel_id=1, source_target_pairs={{0,64},{1,65},{2,66},{3,67},{4,68},{5,69},{6,70},{7,71},{8,72},{9,... | collective-permute-start | bytes 3145736 | tf_op jit(solution)/shard_map/ppermute | solution.py:620
  129.4 77.5 %collective-permute-start.8 = (f32[8,256,128]{2,1,0:T(8,128)}, f32[8,256,128]{2,1,0:T(8,128)}, u32[]{:S(2)}, u32[]{:S(2)}) collective-permute-start(f32[8,256,128]{2,1,0:T(8,128)} %shard_map.86), channel_id=1, source_target_pairs={{0,64},{1,65},{2,66},{3,67},{4,68},{5,69},{6,70},{7,71},{8,72},{9,... | collective-permute-start | bytes 3145736 | tf_op jit(solution)/shard_map/ppermute | solution.py:620
  130.5 51.6 %all-to-all-start.1 = ((f32[64,1,256]{2,1,0:T(1,128)}), f32[64,1,256]{2,1,0:T(1,128)S(1)}, u32[]{:S(2)}, u32[]{:S(2)}) async-start(f32[64,1,256]{2,1,0:T(1,128)} %copy.10), calls=%async_computation.1 | async-start | bytes 131072 | tf_op jit(solution)/shard_map/all_to_all | solution.py:638
  182.7 1.6 copy-start
  206.6 5.7 %collective-permute-start.10 = (f32[64,512]{1,0:T(8,128)}, f32[64,512]{1,0:T(8,128)S(1)}, u32[]{:S(2)}, u32[]{:S(2)}) collective-permute-start(f32[64,512]{1,0:T(8,128)} %get-tuple-element.50), channel_id=1, source_target_pairs={{0,64},{1,65},{2,66},{3,67},{4,68},{5,69},{6,70},{7,71},{8,72},{9,... | collective-permute-start | bytes 393224 | tf_op jit(solution)/shard_map/ppermute | solution.py:647
  212.4 0.7 copy-start.3
